TPU v7x, 256 devices: a whole 4x4x8 slice. The times are simulated.
256 devices in a mesh: gx: 8 (over z), gy: 32 (over x, y, core).
Axes of the slice: x: 4, y: 4, z: 8, core: 2. Of those that a mesh axis runs over, the one named last changes fastest.
Arguments:
- initial_basis: float32 [8, 128, 512, 128], P(None, 'gx', 'gy'), may hold values from 0.1 to 0.5
- labels: int32 [128, 512, 128], P('gx', 'gy'), may hold values from 0 to 15
- class_perm: float32 [16], replicated, may hold values from 0.01 to 100
- support: int32 [128, 512, 128], P('gx', 'gy'), may hold values from 0 to 255
Outputs:
- basis: float32 [8, 128, 512, 128], P(None, 'gx', 'gy')
- coarse: float32 [27, 8, 32, 8], P(None, 'gx', 'gy')
Inputs may be any that keep to these rules, and one draw needn't show every extreme that they name: `support`: bit s of a cell's entry says whether the basis function of its block's corner slot s may be nonzero in that cell.
All inputs are finite; a program needn't handle non-finite values.
Results may differ from a plain program's by a relative error of at most 0.0003.
Values sent between devices are 32-bit elements; how exact they have to be, the bound alone decides.
A program may use at most 64 MiB of HBM per device.

v0:
```python
import numpy as np
import jax
import jax.numpy as jnp
from jax import lax
from jax.experimental import pallas as pl
from jax.experimental.pallas import tpu as pltpu
from jax.sharding import PartitionSpec as P

CB = 16
ITERS = 3
HX = ITERS + 1
HY = ITERS + 1

omega_jacobi = 2.0 / 3.0
renorm_floor = 0.5


def with_halo(block, sides, width):
    for axis, dim in sides:
        count = lax.axis_size(axis)
        forward = [(i, i + 1) for i in range(count - 1)]
        backward = [(target, source) for source, target in forward]
        low = lax.ppermute(
            lax.slice_in_dim(block, block.shape[dim] - width, None, axis=dim), axis, forward
        )
        high = lax.ppermute(lax.slice_in_dim(block, 0, width, axis=dim), axis, backward)
        block = jnp.concatenate([low, block, high], axis=dim)
    return block


def from_behind(shard, axis, by):
    peers = lax.axis_size(axis)
    pairs = [(i, i + by) for i in range(peers) if 0 <= i + by < peers]
    return lax.ppermute(shard, axis, pairs)


def corner_of(slot_index):
    return (slot_index >> 2 & 1, slot_index >> 1 & 1, slot_index & 1)


def conductance(centre, neighbour):
    total_perm = centre + neighbour
    divisor = jnp.where(total_perm > 0.0, total_perm, 1.0)
    return 2.0 * centre * neighbour / divisor


def class_lookup(labels, class_perm):
    classes = jnp.arange(class_perm.shape[0])
    hits = labels[None] == classes[:, None, None, None]
    return jnp.sum(jnp.where(hits, class_perm[:, None, None, None], 0.0), axis=0)


def existing_bits(count_x, count_y, count_z, first_x, first_y, limit_x, limit_y, limit_z):
    block_x = (jnp.arange(count_x) + first_x) // CB
    block_y = (jnp.arange(count_y) + first_y) // CB
    block_z = jnp.arange(count_z) // CB
    bits = jnp.zeros((count_x, count_y, count_z), jnp.int32)
    for slot_index in range(8):
        corner_x, corner_y, corner_z = corner_of(slot_index)
        inside = (
            (block_x + corner_x < limit_x)[:, None, None]
            & (block_y + corner_y < limit_y)[None, :, None]
            & (block_z + corner_z < limit_z)[None, None, :]
        )
        bits = bits | jnp.where(inside, 1 << slot_index, 0)
    return bits


def smooth_kernel(ext_ref, basis_ref, prod_ref, tt, aux, valid, wa, wb, img):
    _, XE, YE, L = ext_ref.shape
    NXL = basis_ref.shape[1]
    NYL = basis_ref.shape[2]
    row = lax.broadcasted_iota(jnp.int32, (YE, L), 0)
    lane = lax.broadcasted_iota(jnp.int32, (YE, L), 1)
    ry = (row + (CB - HY)) & (CB - 1)
    m_yhi = ry == CB - 1
    m_ylo = ry == 0
    rz = lane & (CB - 1)
    m_zhi = rz == CB - 1
    m_zlo = rz == 0
    m_rows = (row >= HY) & (row < HY + NYL)

    def xplace(x):
        return (x + (CB - HX)) & (CB - 1)

    def pre(x, carry):
        pc = ext_ref[8, x]
        pxp = jnp.where(x + 1 < XE, ext_ref[8, jnp.minimum(x + 1, XE - 1)], 0.0)
        pxm = jnp.where(x >= 1, ext_ref[8, jnp.maximum(x - 1, 0)], 0.0)
        pyp = pltpu.roll(pc, YE - 1, 0)
        pym = pltpu.roll(pc, 1, 0)
        pzp = pltpu.roll(pc, L - 1, 1)
        pzm = pltpu.roll(pc, 1, 1)
        t_xp = conductance(pc, pxp)
        t_xm = conductance(pc, pxm)
        t_yp = conductance(pc, pyp)
        t_ym = conductance(pc, pym)
        t_zp = jnp.where(lane == L - 1, 0.0, conductance(pc, pzp))
        t_zm = jnp.where(lane == 0, 0.0, conductance(pc, pzm))
        diag = t_xp + t_xm + t_yp + t_ym + t_zp + t_zm
        aux[0, x] = diag
        aux[1, x] = 1.0 / jnp.where(diag > 0.0, diag, 1.0)
        cx_hi = xplace(x) == CB - 1
        cx_lo = xplace(x) == 0
        tt[0, x] = t_xp
        tt[1, x] = jnp.where(cx_hi, 0.0, t_xp)
        tt[2, x] = t_xm
        tt[3, x] = jnp.where(cx_lo, 0.0, t_xm)
        tt[4, x] = t_yp
        tt[5, x] = jnp.where(m_yhi, 0.0, t_yp)
        tt[6, x] = t_ym
        tt[7, x] = jnp.where(m_ylo, 0.0, t_ym)
        tt[8, x] = t_zp
        tt[9, x] = jnp.where(m_zhi, 0.0, t_zp)
        tt[10, x] = t_zm
        tt[11, x] = jnp.where(m_zlo, 0.0, t_zm)
        sup = ext_ref[9, x].astype(jnp.int32)
        for s in range(8):
            v = ((sup >> s) & 1).astype(jnp.float32)
            valid[s, x] = v
            wa[s, x] = ext_ref[s, x] * v
        return carry

    lax.fori_loop(0, XE, pre, 0)

    def inflow_of(src, x, s, c):
        bx, by, bz = corner_of(s)
        cx_hi = xplace(x) == CB - 1
        cx_lo = xplace(x) == 0
        if bx:
            xp = src[jnp.where(cx_hi, s ^ 4, s), x + 1]
            t1 = tt[0, x]
            xm = src[s, x - 1]
            t2 = tt[3, x]
        else:
            xp = src[s, x + 1]
            t1 = tt[1, x]
            xm = src[jnp.where(cx_lo, s ^ 4, s), x - 1]
            t2 = tt[2, x]
        if by:
            yp = pltpu.roll(jnp.where(m_ylo, src[s ^ 2, x], c), YE - 1, 0)
            t3 = tt[4, x]
            ym = pltpu.roll(c, 1, 0)
            t4 = tt[7, x]
        else:
            yp = pltpu.roll(c, YE - 1, 0)
            t3 = tt[5, x]
            ym = pltpu.roll(jnp.where(m_yhi, src[s ^ 2, x], c), 1, 0)
            t4 = tt[6, x]
        if bz:
            zp = pltpu.roll(jnp.where(m_zlo, src[s ^ 1, x], c), L - 1, 1)
            t5 = tt[8, x]
            zm = pltpu.roll(c, 1, 1)
            t6 = tt[11, x]
        else:
            zp = pltpu.roll(c, L - 1, 1)
            t5 = tt[9, x]
            zm = pltpu.roll(jnp.where(m_zhi, src[s ^ 1, x], c), 1, 1)
            t6 = tt[10, x]
        return t1 * xp + t2 * xm + t3 * yp + t4 * ym + t5 * zp + t6 * zm

    def sweep(src, dst, lo, hi):
        def body(x, carry):
            diag = aux[0, x]
            inv = aux[1, x]
            for s in range(8):
                c = src[s, x]
                inflow = inflow_of(src, x, s, c)
                dst[s, x] = (c - omega_jacobi * (diag * c - inflow) * inv) * valid[s, x]
            return carry

        lax.fori_loop(lo, hi, body, 0)

    bufs = (wa, wb)
    for step in range(ITERS):
        sweep(bufs[step % 2], bufs[(step + 1) % 2], step + 1, XE - step - 1)
    last = bufs[ITERS % 2]
    basis_buf = bufs[(ITERS + 1) % 2]

    def normalize(x, carry):
        vals = [last[s, x] for s in range(8)]
        total = vals[0]
        for s in range(1, 8):
            total = total + vals[s]
        scale = jnp.maximum(total, renorm_floor)
        for s in range(8):
            basis_buf[s, x] = vals[s] / scale
        return carry

    lax.fori_loop(ITERS, XE - ITERS, normalize, 0)

    def image(x, carry):
        diag = aux[0, x]
        for s in range(8):
            c = basis_buf[s, x]
            inflow = inflow_of(basis_buf, x, s, c)
            img[s, x - HX] = jnp.where(m_rows, diag * c - inflow, 0.0)
            basis_ref[s, x - HX] = c[HY:HY + NYL, :]
        return carry

    lax.fori_loop(HX, HX + NXL, image, 0)

    for s1 in range(8):
        def pair_sums(x, acc):
            b = basis_buf[s1, x + HX]
            return tuple(acc[s2] + b * img[s2, x] for s2 in range(8))

        acc = lax.fori_loop(
            0, NXL, pair_sums, tuple(jnp.zeros((YE, L), jnp.float32) for _ in range(8))
        )
        for s2 in range(8):
            prod_ref[pl.ds(s1 * 8 + s2, 1), :] = jnp.sum(acc[s2], axis=0, keepdims=True)


def assembly_matrix():
    table = np.zeros((4 * 27 * 2, 64), np.float32)
    for first_slot in range(8):
        for second_slot in range(8):
            one_x, one_y, one_z = corner_of(first_slot)
            two_x, two_y, two_z = corner_of(second_slot)
            offset_index = 9 * (two_x - one_x + 1) + 3 * (two_y - one_y + 1) + (two_z - one_z + 1)
            row = ((one_x * 2 + one_y) * 27 + offset_index) * 2 + one_z
            table[row, first_slot * 8 + second_slot] = 1.0
    return table


def shards(initial_basis, labels, class_perm, support):
    size_x, size_y, size_z = labels.shape
    assert size_x == CB and size_y == CB and size_z % CB == 0
    blocks_z = size_z // CB
    permeability = class_lookup(labels, class_perm)
    keep = existing_bits(
        size_x,
        size_y,
        size_z,
        lax.axis_index("gx") * size_x,
        lax.axis_index("gy") * size_y,
        lax.axis_size("gx") * size_x // CB,
        lax.axis_size("gy") * size_y // CB,
        blocks_z,
    )
    support_f = (support & keep).astype(jnp.float32)
    packed = jnp.concatenate([initial_basis, permeability[None], support_f[None]], axis=0)
    ext = with_halo(packed, (("gx", 1), ("gy", 2)), HX)
    XE, YE = size_x + 2 * HX, size_y + 2 * HY
    f32 = jnp.float32
    basis, prods = pl.pallas_call(
        smooth_kernel,
        out_shape=(
            jax.ShapeDtypeStruct((8, size_x, size_y, size_z), f32),
            jax.ShapeDtypeStruct((64, size_z), f32),
        ),
        in_specs=[pl.BlockSpec(memory_space=pltpu.VMEM)],
        out_specs=(pl.BlockSpec(memory_space=pltpu.VMEM), pl.BlockSpec(memory_space=pltpu.VMEM)),
        scratch_shapes=[
            pltpu.VMEM((12, XE, YE, size_z), f32),
            pltpu.VMEM((2, XE, YE, size_z), f32),
            pltpu.VMEM((8, XE, YE, size_z), f32),
            pltpu.VMEM((8, XE, YE, size_z), f32),
            pltpu.VMEM((8, XE, YE, size_z), f32),
            pltpu.VMEM((8, size_x, YE, size_z), f32),
        ],
    )(ext)
    block_sums = prods.reshape(64, blocks_z, CB).sum(axis=-1)
    placed = jnp.dot(
        jnp.asarray(assembly_matrix()), block_sums, precision=lax.Precision.HIGHEST
    ).reshape(4, 27, 2, blocks_z)
    contrib = placed[:, :, 0] + jnp.pad(placed[:, :, 1, :-1], ((0, 0), (0, 0), (1, 0)))
    nx = lax.axis_size("gx")
    ny = lax.axis_size("gy")
    from_x = from_behind(contrib[2], "gx", 1)
    from_y = from_behind(contrib[1], "gy", 1)
    diagonal_pairs = [
        (i * ny + j, (i + 1) * ny + j + 1) for i in range(nx - 1) for j in range(ny - 1)
    ]
    from_xy = lax.ppermute(contrib[3], ("gx", "gy"), diagonal_pairs)
    owned = contrib[0] + from_x + from_y + from_xy
    return (basis, owned.reshape(27, 1, 1, blocks_z))


def solution(mesh):
    return jax.shard_map(
        shards,
        mesh=mesh,
        in_specs=(P(None, "gx", "gy", None), P("gx", "gy", None), P(), P("gx", "gy", None)),
        out_specs=(P(None, "gx", "gy", None), P(None, "gx", "gy", None)),
        check_vma=False,
    )
```

profile of v0, /device:TPU:34, one launch (start us, length us, event | category | flops | bytes accessed | tf_op | source)
XLA Modules:
  0.0 71.3 jit_solution(779380092656855605)
XLA Ops:
  0.6 0.0 copy-start
  0.7 1.3 %select_reduce_fusion = f32[16,16,128]{2,1,0:T(8,128)S(1)} fusion(f32[16]{0:T(128)} %param.7, s32[16,16,128]{2,1,0:T(8,128)} %param.6), kind=kLoop, calls=%fused_computation.1 | loop fusion | flops 1540096 | bytes 262208 | tf_op jit(solution)/shard_map/reduce_sum | solution.py:50
  2.0 0.1 broadcast_and_fusion.3
  2.1 1.1 %convert_bitcast_fusion = f32[1,16,16,128]{3,2,1,0:T(8,128)S(1)} fusion(s32[16,16,128]{2,1,0:T(8,128)} %param.8, pred[16,16]{1,0:T(8,128)(4,1)S(1)} %get-tuple-element.19, pred[16,16]{1,0:T(8,128)(4,1)S(1)} %get-tuple-element.20, pred[16,16]{1,0:T(8,128)(4,1)S(1)} %get-tuple-element.18, pred[128]{0:T(512)(128)(4,1)S(1)} %get-tuple-element.25, ...), kind=kLoop, calls=%fused_computation.11 | loop fusion | flops 819200 | bytes 263424 | tf_op jit(solution)/shard_map/broadcast_in_dim | solution.py:243
  3.2 1.1 %pad_maximum_fusion.8 = (f32[10,4,16,128]{3,2,1,0:T(8,128)S(1)}, f32[10,4,16,128]{3,2,1,0:T(8,128)S(1)}) fusion(f32[1,16,16,128]{3,2,1,0:T(8,128)S(1)} %convert_bitcast_fusion, f32[1,16,16,128]{3,2,1,0:T(8,128)S(1)} %bitcast.29, f32[8,16,16,128]{3,2,1,0:T(8,128)} %param.5), kind=kLoop, calls=%fused_computation.10 | loop fusion | flops 327680 | bytes 1966080 | tf_op jit(solution)/shard_map/slice | solution.py:24
  4.3 3.8 %collective-permute-start = (f32[10,4,16,128]{3,2,1,0:T(8,128)S(1)}, f32[10,4,16,128]{3,2,1,0:T(8,128)S(1)}, u32[]{:S(2)}, u32[]{:S(2)}) collective-permute-start(f32[10,4,16,128]{3,2,1,0:T(8,128)S(1)} %get-tuple-element.12), channel_id=1, source_target_pairs={{0,32},{32,64},{64,96},{96,128},{128,160},{160,192},{192,224},{1,3... | collective-permute-start | bytes 983048 | tf_op jit(solution)/shard_map/ppermute | solution.py:23
  8.1 2.0 %collective-permute-start.1 = (f32[10,4,16,128]{3,2,1,0:T(8,128)S(1)}, f32[10,4,16,128]{3,2,1,0:T(8,128)S(1)}, u32[]{:S(2)}, u32[]{:S(2)}) collective-permute-start(f32[10,4,16,128]{3,2,1,0:T(8,128)S(1)} %get-tuple-element.13), channel_id=1, source_target_pairs={{32,0},{64,32},{96,64},{128,96},{160,128},{192,160},{224,192},{33,... | collective-permute-start | bytes 983048 | tf_op jit(solution)/shard_map/ppermute | solution.py:26
  10.1 5.5 %collective-permute-done = f32[10,4,16,128]{3,2,1,0:T(8,128)S(1)} collective-permute-done((f32[10,4,16,128]{3,2,1,0:T(8,128)S(1)}, f32[10,4,16,128]{3,2,1,0:T(8,128)S(1)}, u32[]{:S(2)}, u32[]{:S(2)}) %collective-permute-start) | collective-permute-done | bytes 327712 | tf_op jit(solution)/shard_map/ppermute | solution.py:23
  15.6 3.7 %collective-permute-done.1 = f32[10,4,16,128]{3,2,1,0:T(8,128)S(1)} collective-permute-done((f32[10,4,16,128]{3,2,1,0:T(8,128)S(1)}, f32[10,4,16,128]{3,2,1,0:T(8,128)S(1)}, u32[]{:S(2)}, u32[]{:S(2)}) %collective-permute-start.1) | collective-permute-done | bytes 327712 | tf_op jit(solution)/shard_map/ppermute | solution.py:26
  19.4 0.0 copy-done
  19.4 0.2 pad_maximum_fusion.5
  19.6 1.9 %collective-permute-start.2 = (f32[10,24,4,128]{3,2,1,0:T(4,128)S(1)}, f32[10,24,4,128]{3,2,1,0:T(4,128)S(1)}, u32[]{:S(2)}, u32[]{:S(2)}) collective-permute-start(f32[10,24,4,128]{3,2,1,0:T(4,128)S(1)} %get-tuple-element.10), channel_id=1, source_target_pairs={{0,1},{1,2},{2,3},{3,4},{4,5},{5,6},{6,7},{7,8},{8,9},{9,10},{10,1... | collective-permute-start | bytes 1474568 | tf_op jit(solution)/shard_map/ppermute | solution.py:23
  21.5 5.8 %collective-permute-start.3 = (f32[10,24,4,128]{3,2,1,0:T(4,128)S(1)}, f32[10,24,4,128]{3,2,1,0:T(4,128)S(1)}, u32[]{:S(2)}, u32[]{:S(2)}) collective-permute-start(f32[10,24,4,128]{3,2,1,0:T(4,128)S(1)} %get-tuple-element.11), channel_id=1, source_target_pairs={{1,0},{2,1},{3,2},{4,3},{5,4},{6,5},{7,6},{8,7},{9,8},{10,9},{11,1... | collective-permute-start | bytes 1474568 | tf_op jit(solution)/shard_map/ppermute | solution.py:26
  27.3 4.6 %collective-permute-done.2 = f32[10,24,4,128]{3,2,1,0:T(4,128)S(1)} collective-permute-done((f32[10,24,4,128]{3,2,1,0:T(4,128)S(1)}, f32[10,24,4,128]{3,2,1,0:T(4,128)S(1)}, u32[]{:S(2)}, u32[]{:S(2)}) %collective-permute-start.2) | collective-permute-done | bytes 491552 | tf_op jit(solution)/shard_map/ppermute | solution.py:23
  31.9 1.8 %collective-permute-done.3 = f32[10,24,4,128]{3,2,1,0:T(4,128)S(1)} collective-permute-done((f32[10,24,4,128]{3,2,1,0:T(4,128)S(1)}, f32[10,24,4,128]{3,2,1,0:T(4,128)S(1)}, u32[]{:S(2)}, u32[]{:S(2)}) %collective-permute-start.3) | collective-permute-done | bytes 491552 | tf_op jit(solution)/shard_map/ppermute | solution.py:26
  33.6 2.1 %pad_maximum_fusion.ext_ref = f32[10,24,24,128]{3,2,1,0:T(8,128)} fusion(f32[10,24,4,128]{3,2,1,0:T(4,128)S(1)} %collective-permute-done.3, f32[10,4,16,128]{3,2,1,0:T(8,128)S(1)} %collective-permute-done.1, f32[1,16,16,128]{3,2,1,0:T(8,128)S(1)} %convert_bitcast_fusion, f32[1,16,16,128]{3,2,1,0:T(8,128)S(1)} %bitcast.31, f32[8,16,16,128]{3,2,1,0:T(8,128)S(1)} %copy-done, ...), kind=kLoop, calls=%fused_computation | loop fusion | flops 4423680 | bytes 5898240 | tf_op jit(solution)/shard_map/concatenate | solution.py:27
  35.7 0.0 copy-start.1
  35.7 17.0 %shard_map.68 = (f32[8,16,16,128]{3,2,1,0:T(8,128)}, f32[64,128]{1,0:T(8,128)}) custom-call(f32[10,24,24,128]{3,2,1,0:T(8,128)} %pad_maximum_fusion.ext_ref), custom_call_target="tpu_custom_call" | custom-call | tf_op jit(solution)/shard_map/pallas_call | solution.py:247
  52.7 0.8 %copy.28 = f32[64,128]{0,1:T(8,128)S(1)} copy(f32[64,128]{1,0:T(8,128)} %get-tuple-element.5) | data formatting | bytes 65536 | tf_op jit(solution)/shard_map/pallas_call | solution.py:247
  53.6 0.0 copy-done.1
  53.6 0.3 fusion.4
  53.9 0.1 slice.41
  54.1 0.1 copy.31
  54.2 0.1 copy.30
  54.3 5.0 %collective-permute-start.4 = (f32[27,8]{0,1:T(8,128)S(1)}, f32[27,8]{0,1:T(8,128)S(1)}, u32[]{:S(2)}, u32[]{:S(2)}) collective-permute-start(f32[27,8]{0,1:T(8,128)S(1)} %get-tuple-element.14), channel_id=1, source_target_pairs={{0,32},{32,64},{64,96},{96,128},{128,160},{160,192},{192,224},{1,3... | collective-permute-start | bytes 2600 | tf_op jit(solution)/shard_map/ppermute | solution.py:34
  59.3 3.9 %collective-permute-start.6 = (f32[27,8]{0,1:T(8,128)S(1)}, f32[27,8]{0,1:T(8,128)S(1)}, u32[]{:S(2)}, u32[]{:S(2)}) collective-permute-start(f32[27,8]{0,1:T(8,128)S(1)} %get-tuple-element.15), channel_id=1, source_target_pairs={{0,33},{1,34},{2,35},{3,36},{4,37},{5,38},{6,39},{7,40},{8,41},{9,... | collective-permute-start | bytes 2600 | tf_op jit(solution)/shard_map/ppermute | solution.py:276
  63.3 1.9 %collective-permute-start.5 = (f32[27,8]{0,1:T(8,128)S(1)}, f32[27,8]{0,1:T(8,128)S(1)}, u32[]{:S(2)}, u32[]{:S(2)}) collective-permute-start(f32[27,8]{0,1:T(8,128)S(1)} %get-tuple-element.16), channel_id=1, source_target_pairs={{0,1},{1,2},{2,3},{3,4},{4,5},{5,6},{6,7},{7,8},{8,9},{9,10},{10,1... | collective-permute-start | bytes 2600 | tf_op jit(solution)/shard_map/ppermute | solution.py:34
  65.2 0.0 collective-permute-done.4
  65.2 2.1 %collective-permute-done.6 = f32[27,8]{0,1:T(8,128)S(1)} collective-permute-done((f32[27,8]{0,1:T(8,128)S(1)}, f32[27,8]{0,1:T(8,128)S(1)}, u32[]{:S(2)}, u32[]{:S(2)}) %collective-permute-start.6) | collective-permute-done | bytes 896 | tf_op jit(solution)/shard_map/ppermute | solution.py:276
  67.3 3.4 %collective-permute-done.5 = f32[27,8]{0,1:T(8,128)S(1)} collective-permute-done((f32[27,8]{0,1:T(8,128)S(1)}, f32[27,8]{0,1:T(8,128)S(1)}, u32[]{:S(2)}, u32[]{:S(2)}) %collective-permute-start.5) | collective-permute-done | bytes 896 | tf_op jit(solution)/shard_map/ppermute | solution.py:34
  70.7 0.6 fusion.3
  (8 shorter events, 0.1 us)
Async XLA Ops:
  0.6 18.7 %copy-start = (f32[8,16,16,128]{3,2,1,0:T(8,128)S(1)}, f32[8,16,16,128]{3,2,1,0:T(8,128)}, u32[]{:S(2)}) copy-start(f32[8,16,16,128]{3,2,1,0:T(8,128)} %param.5) | copy-start | bytes 3145732
  4.3 11.3 %collective-permute-start = (f32[10,4,16,128]{3,2,1,0:T(8,128)S(1)}, f32[10,4,16,128]{3,2,1,0:T(8,128)S(1)}, u32[]{:S(2)}, u32[]{:S(2)}) collective-permute-start(f32[10,4,16,128]{3,2,1,0:T(8,128)S(1)} %get-tuple-element.12), channel_id=1, source_target_pairs={{0,32},{32,64},{64,96},{96,128},{128,160},{160,192},{192,224},{1,3... | collective-permute-start | bytes 983048 | tf_op jit(solution)/shard_map/ppermute | solution.py:23
  8.1 11.2 %collective-permute-start.1 = (f32[10,4,16,128]{3,2,1,0:T(8,128)S(1)}, f32[10,4,16,128]{3,2,1,0:T(8,128)S(1)}, u32[]{:S(2)}, u32[]{:S(2)}) collective-permute-start(f32[10,4,16,128]{3,2,1,0:T(8,128)S(1)} %get-tuple-element.13), channel_id=1, source_target_pairs={{32,0},{64,32},{96,64},{128,96},{160,128},{192,160},{224,192},{33,... | collective-permute-start | bytes 983048 | tf_op jit(solution)/shard_map/ppermute | solution.py:26
  19.6 12.3 %collective-permute-start.2 = (f32[10,24,4,128]{3,2,1,0:T(4,128)S(1)}, f32[10,24,4,128]{3,2,1,0:T(4,128)S(1)}, u32[]{:S(2)}, u32[]{:S(2)}) collective-permute-start(f32[10,24,4,128]{3,2,1,0:T(4,128)S(1)} %get-tuple-element.10), channel_id=1, source_target_pairs={{0,1},{1,2},{2,3},{3,4},{4,5},{5,6},{6,7},{7,8},{8,9},{9,10},{10,1... | collective-permute-start | bytes 1474568 | tf_op jit(solution)/shard_map/ppermute | solution.py:23
  21.5 12.1 %collective-permute-start.3 = (f32[10,24,4,128]{3,2,1,0:T(4,128)S(1)}, f32[10,24,4,128]{3,2,1,0:T(4,128)S(1)}, u32[]{:S(2)}, u32[]{:S(2)}) collective-permute-start(f32[10,24,4,128]{3,2,1,0:T(4,128)S(1)} %get-tuple-element.11), channel_id=1, source_target_pairs={{1,0},{2,1},{3,2},{4,3},{5,4},{6,5},{7,6},{8,7},{9,8},{10,9},{11,1... | collective-permute-start | bytes 1474568 | tf_op jit(solution)/shard_map/ppermute | solution.py:26
  35.7 17.9 %copy-start.1 = (f32[216,64]{1,0:T(8,128)S(1)}, f32[216,64]{1,0:T(8,128)}, u32[]{:S(2)}) copy-start(f32[216,64]{1,0:T(8,128)} %constant.69.clone) | copy-start | bytes 165892
  54.3 10.9 %collective-permute-start.4 = (f32[27,8]{0,1:T(8,128)S(1)}, f32[27,8]{0,1:T(8,128)S(1)}, u32[]{:S(2)}, u32[]{:S(2)}) collective-permute-start(f32[27,8]{0,1:T(8,128)S(1)} %get-tuple-element.14), channel_id=1, source_target_pairs={{0,32},{32,64},{64,96},{96,128},{128,160},{160,192},{192,224},{1,3... | collective-permute-start | bytes 2600 | tf_op jit(solution)/shard_map/ppermute | solution.py:34
  59.3 7.9 %collective-permute-start.6 = (f32[27,8]{0,1:T(8,128)S(1)}, f32[27,8]{0,1:T(8,128)S(1)}, u32[]{:S(2)}, u32[]{:S(2)}) collective-permute-start(f32[27,8]{0,1:T(8,128)S(1)} %get-tuple-element.15), channel_id=1, source_target_pairs={{0,33},{1,34},{2,35},{3,36},{4,37},{5,38},{6,39},{7,40},{8,41},{9,... | collective-permute-start | bytes 2600 | tf_op jit(solution)/shard_map/ppermute | solution.py:276
  63.3 7.4 %collective-permute-start.5 = (f32[27,8]{0,1:T(8,128)S(1)}, f32[27,8]{0,1:T(8,128)S(1)}, u32[]{:S(2)}, u32[]{:S(2)}) collective-permute-start(f32[27,8]{0,1:T(8,128)S(1)} %get-tuple-element.16), channel_id=1, source_target_pairs={{0,1},{1,2},{2,3},{3,4},{4,5},{5,6},{6,7},{7,8},{8,9},{9,10},{10,1... | collective-permute-start | bytes 2600 | tf_op jit(solution)/shard_map/ppermute | solution.py:34
where the time goes:
time: 71.7 us; the launch traced here: 71.3 us
  starting transfers between devices  24.4 us (34%)
  waiting for transfers between devices  21 us (29%)
  Pallas kernels  17 us (24%)
  other arithmetic  6.57 us (9%)
  local copies, waits for them, and re-layouts  1.16 us (2%)
  between operations  0.81 us (1%)
    pallas_call x1, Pallas kernels, shards(): pl.pallas_call(smooth_kernel, out_shape=(jax.ShapeDtypeStruct((8, size_x,...  17 us
    ppermute x2, waiting for transfers between devices, with_halo(): lax.ppermute(lax.slice_in_dim(block, block.shape[dim] - width, None, axis...  10 us
    ppermute x2, starting transfers between devices, with_halo(): lax.ppermute(lax.slice_in_dim(block, 0, width, axis=dim), axis, backward)  7.78 us
    ppermute x2, starting transfers between devices, from_behind(): return lax.ppermute(shard, axis, pairs)  6.96 us
    ppermute x2, starting transfers between devices, with_halo(): lax.ppermute(lax.slice_in_dim(block, block.shape[dim] - width, None, axis...  5.75 us
    ppermute x2, waiting for transfers between devices, with_halo(): lax.ppermute(lax.slice_in_dim(block, 0, width, axis=dim), axis, backward)  5.49 us
    ppermute x1, starting transfers between devices, shards(): from_xy = lax.ppermute(contrib[3], ('gx', 'gy'), diagonal_pairs)  3.93 us
    ppermute x2, waiting for transfers between devices, from_behind(): return lax.ppermute(shard, axis, pairs)  3.42 us
  transfers between devices with their start and end apart: 7, of which 6 were waited for; matrix products, arithmetic and copies ran while one was open for 0% of the time, Pallas kernels for 0%

commit v1 on v0

--- a/solution.py
+++ b/solution.py
@@ -1,3 +1,4 @@
+import functools
 import numpy as np
 import jax
 import jax.numpy as jnp
@@ -266,16 +267,80 @@
         jnp.asarray(assembly_matrix()), block_sums, precision=lax.Precision.HIGHEST
     ).reshape(4, 27, 2, blocks_z)
     contrib = placed[:, :, 0] + jnp.pad(placed[:, :, 1, :-1], ((0, 0), (0, 0), (1, 0)))
-    nx = lax.axis_size("gx")
-    ny = lax.axis_size("gy")
-    from_x = from_behind(contrib[2], "gx", 1)
-    from_y = from_behind(contrib[1], "gy", 1)
-    diagonal_pairs = [
-        (i * ny + j, (i + 1) * ny + j + 1) for i in range(nx - 1) for j in range(ny - 1)
-    ]
-    from_xy = lax.ppermute(contrib[3], ("gx", "gy"), diagonal_pairs)
-    owned = contrib[0] + from_x + from_y + from_xy
+    owned = exchange_coarse(contrib, lax.axis_size("gx"), lax.axis_size("gy"))
     return (basis, owned.reshape(27, 1, 1, blocks_z))
+
+
+def coarse_kernel(nx, ny, c_ref, o_ref, recv, send_sem, recv_sem):
+    i = lax.axis_index("gx")
+    j = lax.axis_index("gy")
+    mesh_id = pl.DeviceIdType.MESH
+    recv[...] = jnp.zeros_like(recv)
+    routes = ((2, 0, 1, 0), (1, 1, 0, 1), (3, 2, 1, 1))
+    barrier = pltpu.get_barrier_semaphore()
+    for _, _, dx, dy in routes:
+        has_dst = (i + dx < nx) & (j + dy < ny)
+        has_src = (i - dx >= 0) & (j - dy >= 0)
+
+        @pl.when(has_dst)
+        def _():
+            pl.semaphore_signal(barrier, 1, device_id=(i + dx, j + dy), device_id_type=mesh_id)
+
+        @pl.when(has_src)
+        def _():
+            pl.semaphore_signal(barrier, 1, device_id=(i - dx, j - dy), device_id_type=mesh_id)
+
+    peers = jnp.int32(0)
+    for _, _, dx, dy in routes:
+        has_dst = (i + dx < nx) & (j + dy < ny)
+        has_src = (i - dx >= 0) & (j - dy >= 0)
+        peers = peers + has_dst.astype(jnp.int32) + has_src.astype(jnp.int32)
+    pl.semaphore_wait(barrier, peers)
+
+    copies = []
+    for slot, k, dx, dy in routes:
+        has_dst = (i + dx < nx) & (j + dy < ny)
+        has_src = (i - dx >= 0) & (j - dy >= 0)
+        out_copy = pltpu.make_async_remote_copy(
+            src_ref=c_ref.at[slot],
+            dst_ref=recv.at[k],
+            send_sem=send_sem.at[k],
+            recv_sem=recv_sem.at[k],
+            device_id=(jnp.minimum(i + dx, nx - 1), jnp.minimum(j + dy, ny - 1)),
+            device_id_type=mesh_id,
+        )
+        copies.append((out_copy, has_dst, has_src))
+
+        @pl.when(has_dst)
+        def _():
+            out_copy.start()
+
+    for out_copy, has_dst, has_src in copies:
+        @pl.when(has_dst)
+        def _():
+            out_copy.wait_send()
+
+        @pl.when(has_src)
+        def _():
+            out_copy.wait_recv()
+
+    o_ref[...] = c_ref[0] + recv[0] + recv[1] + recv[2]
+
+
+def exchange_coarse(contrib, nx, ny):
+    _, rows, cols = contrib.shape
+    return pl.pallas_call(
+        functools.partial(coarse_kernel, nx, ny),
+        out_shape=jax.ShapeDtypeStruct((rows, cols), jnp.float32),
+        in_specs=[pl.BlockSpec(memory_space=pltpu.VMEM)],
+        out_specs=pl.BlockSpec(memory_space=pltpu.VMEM),
+        scratch_shapes=[
+            pltpu.VMEM((3, rows, cols), jnp.float32),
+            pltpu.SemaphoreType.DMA((3,)),
+            pltpu.SemaphoreType.DMA((3,)),
+        ],
+        compiler_params=pltpu.CompilerParams(collective_id=0, has_side_effects=True),
+    )(contrib)
 
 
 def solution(mesh):

time: 71.7 us -> 67.4 us (0.940)
  the two profiles are of different devices: /device:TPU:34 before, /device:TPU:70 now
where the time goes in v1:
time: 67.4 us; the launch traced here: 67 us
  Pallas kernels  26.6 us (39%)
  waiting for transfers between devices  16.8 us (25%)
  starting transfers between devices  13.5 us (20%)
  other arithmetic  6.67 us (10%)
  local copies, waits for them, and re-layouts  2.34 us (3%)
  between operations  0.79 us (1%)
    pallas_call x1, Pallas kernels, shards(): pl.pallas_call(smooth_kernel, out_shape=(jax.ShapeDtypeStruct((8, size_x,...  17 us
    ppermute x2, waiting for transfers between devices, with_halo(): lax.ppermute(lax.slice_in_dim(block, block.shape[dim] - width, None, axis...  10.1 us
    pallas_call x1, Pallas kernels, exchange_coarse(): pl.pallas_call(functools.partial(coarse_kernel, nx, ny), out_shape=jax.Sh...  9.58 us
    ppermute x2, starting transfers between devices, with_halo(): lax.ppermute(lax.slice_in_dim(block, 0, width, axis=dim), axis, backward)  7.77 us
    ppermute x2, waiting for transfers between devices, with_halo(): lax.ppermute(lax.slice_in_dim(block, 0, width, axis=dim), axis, backward)  6.7 us
    ppermute x2, starting transfers between devices, with_halo(): lax.ppermute(lax.slice_in_dim(block, block.shape[dim] - width, None, axis...  5.75 us
    concatenate x1, other arithmetic, with_halo(): block = jnp.concatenate([low, block, high], axis=dim)  2.11 us
    unnamed x6, local copies, waits for them, and re-layouts  1.4 us
  transfers between devices with their start and end apart: 4, of which 4 were waited for; matrix products, arithmetic and copies ran while one was open for 0% of the time, Pallas kernels for 0%

profile of v1, /device:TPU:70, one launch (start us, length us, event | category | flops | bytes accessed | tf_op | source)
XLA Modules:
  0.0 67.0 jit_solution(16350711172076870390)
XLA Ops:
  0.6 0.0 copy-start
  0.7 1.3 %select_reduce_fusion = f32[16,16,128]{2,1,0:T(8,128)S(1)} fusion(f32[16]{0:T(128)} %param.7, s32[16,16,128]{2,1,0:T(8,128)} %param.6), kind=kLoop, calls=%fused_computation.1 | loop fusion | flops 1540096 | bytes 262208 | tf_op jit(solution)/shard_map/reduce_sum | solution.py:51
  2.0 0.1 broadcast_and_fusion.3
  2.1 1.1 %convert_bitcast_fusion = f32[1,16,16,128]{3,2,1,0:T(8,128)S(1)} fusion(s32[16,16,128]{2,1,0:T(8,128)} %param.8, pred[16,16]{1,0:T(8,128)(4,1)S(1)} %get-tuple-element.20, pred[16,16]{1,0:T(8,128)(4,1)S(1)} %get-tuple-element.21, pred[16,16]{1,0:T(8,128)(4,1)S(1)} %get-tuple-element.19, pred[128]{0:T(512)(128)(4,1)S(1)} %get-tuple-element.26, ...), kind=kLoop, calls=%fused_computation.11 | loop fusion | flops 819200 | bytes 263424 | tf_op jit(solution)/shard_map/broadcast_in_dim | solution.py:244
  3.2 1.1 %pad_maximum_fusion.8 = (f32[10,4,16,128]{3,2,1,0:T(8,128)S(1)}, f32[10,4,16,128]{3,2,1,0:T(8,128)S(1)}) fusion(f32[1,16,16,128]{3,2,1,0:T(8,128)S(1)} %convert_bitcast_fusion, f32[1,16,16,128]{3,2,1,0:T(8,128)S(1)} %bitcast.16, f32[8,16,16,128]{3,2,1,0:T(8,128)} %param.5), kind=kLoop, calls=%fused_computation.10 | loop fusion | flops 327680 | bytes 1966080 | tf_op jit(solution)/shard_map/slice | solution.py:25
  4.3 3.8 %collective-permute-start = (f32[10,4,16,128]{3,2,1,0:T(8,128)S(1)}, f32[10,4,16,128]{3,2,1,0:T(8,128)S(1)}, u32[]{:S(2)}, u32[]{:S(2)}) collective-permute-start(f32[10,4,16,128]{3,2,1,0:T(8,128)S(1)} %get-tuple-element.16), channel_id=1, source_target_pairs={{0,32},{32,64},{64,96},{96,128},{128,160},{160,192},{192,224},{1,3... | collective-permute-start | bytes 983048 | tf_op jit(solution)/shard_map/ppermute | solution.py:24
  8.1 2.0 %collective-permute-start.1 = (f32[10,4,16,128]{3,2,1,0:T(8,128)S(1)}, f32[10,4,16,128]{3,2,1,0:T(8,128)S(1)}, u32[]{:S(2)}, u32[]{:S(2)}) collective-permute-start(f32[10,4,16,128]{3,2,1,0:T(8,128)S(1)} %get-tuple-element.17), channel_id=1, source_target_pairs={{32,0},{64,32},{96,64},{128,96},{160,128},{192,160},{224,192},{33,... | collective-permute-start | bytes 983048 | tf_op jit(solution)/shard_map/ppermute | solution.py:27
  10.1 5.5 %collective-permute-done = f32[10,4,16,128]{3,2,1,0:T(8,128)S(1)} collective-permute-done((f32[10,4,16,128]{3,2,1,0:T(8,128)S(1)}, f32[10,4,16,128]{3,2,1,0:T(8,128)S(1)}, u32[]{:S(2)}, u32[]{:S(2)}) %collective-permute-start) | collective-permute-done | bytes 327712 | tf_op jit(solution)/shard_map/ppermute | solution.py:24
  15.6 4.9 %collective-permute-done.1 = f32[10,4,16,128]{3,2,1,0:T(8,128)S(1)} collective-permute-done((f32[10,4,16,128]{3,2,1,0:T(8,128)S(1)}, f32[10,4,16,128]{3,2,1,0:T(8,128)S(1)}, u32[]{:S(2)}, u32[]{:S(2)}) %collective-permute-start.1) | collective-permute-done | bytes 327712 | tf_op jit(solution)/shard_map/ppermute | solution.py:27
  20.6 0.0 copy-done
  20.6 0.2 pad_maximum_fusion.5
  20.8 1.9 %collective-permute-start.2 = (f32[10,24,4,128]{3,2,1,0:T(4,128)S(1)}, f32[10,24,4,128]{3,2,1,0:T(4,128)S(1)}, u32[]{:S(2)}, u32[]{:S(2)}) collective-permute-start(f32[10,24,4,128]{3,2,1,0:T(4,128)S(1)} %get-tuple-element.14), channel_id=1, source_target_pairs={{0,1},{1,2},{2,3},{3,4},{4,5},{5,6},{6,7},{7,8},{8,9},{9,10},{10,1... | collective-permute-start | bytes 1474568 | tf_op jit(solution)/shard_map/ppermute | solution.py:24
  22.7 5.8 %collective-permute-start.3 = (f32[10,24,4,128]{3,2,1,0:T(4,128)S(1)}, f32[10,24,4,128]{3,2,1,0:T(4,128)S(1)}, u32[]{:S(2)}, u32[]{:S(2)}) collective-permute-start(f32[10,24,4,128]{3,2,1,0:T(4,128)S(1)} %get-tuple-element.15), channel_id=1, source_target_pairs={{1,0},{2,1},{3,2},{4,3},{5,4},{6,5},{7,6},{8,7},{9,8},{10,9},{11,1... | collective-permute-start | bytes 1474568 | tf_op jit(solution)/shard_map/ppermute | solution.py:27
  28.5 4.6 %collective-permute-done.2 = f32[10,24,4,128]{3,2,1,0:T(4,128)S(1)} collective-permute-done((f32[10,24,4,128]{3,2,1,0:T(4,128)S(1)}, f32[10,24,4,128]{3,2,1,0:T(4,128)S(1)}, u32[]{:S(2)}, u32[]{:S(2)}) %collective-permute-start.2) | collective-permute-done | bytes 491552 | tf_op jit(solution)/shard_map/ppermute | solution.py:24
  33.1 1.8 %collective-permute-done.3 = f32[10,24,4,128]{3,2,1,0:T(4,128)S(1)} collective-permute-done((f32[10,24,4,128]{3,2,1,0:T(4,128)S(1)}, f32[10,24,4,128]{3,2,1,0:T(4,128)S(1)}, u32[]{:S(2)}, u32[]{:S(2)}) %collective-permute-start.3) | collective-permute-done | bytes 491552 | tf_op jit(solution)/shard_map/ppermute | solution.py:27
  34.8 2.1 %pad_maximum_fusion.ext_ref = f32[10,24,24,128]{3,2,1,0:T(8,128)} fusion(f32[10,24,4,128]{3,2,1,0:T(4,128)S(1)} %collective-permute-done.3, f32[10,4,16,128]{3,2,1,0:T(8,128)S(1)} %collective-permute-done.1, f32[1,16,16,128]{3,2,1,0:T(8,128)S(1)} %convert_bitcast_fusion, f32[1,16,16,128]{3,2,1,0:T(8,128)S(1)} %bitcast.18, f32[8,16,16,128]{3,2,1,0:T(8,128)S(1)} %copy-done, ...), kind=kLoop, calls=%fused_computation | loop fusion | flops 4423680 | bytes 5898240 | tf_op jit(solution)/shard_map/concatenate | solution.py:28
  36.9 0.0 copy-start.1
  36.9 17.0 %shard_map.68 = (f32[8,16,16,128]{3,2,1,0:T(8,128)}, f32[64,128]{1,0:T(8,128)}) custom-call(f32[10,24,24,128]{3,2,1,0:T(8,128)} %pad_maximum_fusion.ext_ref), custom_call_target="tpu_custom_call" | custom-call | tf_op jit(solution)/shard_map/pallas_call | solution.py:248
  54.0 0.8 %copy.18 = f32[64,128]{0,1:T(8,128)S(1)} copy(f32[64,128]{1,0:T(8,128)} %get-tuple-element.5) | data formatting | bytes 65536 | tf_op jit(solution)/shard_map/pallas_call | solution.py:248
  54.8 0.0 copy-done.1
  54.8 0.3 fusion.1
  55.2 0.1 slice.25
  55.3 0.7 %fusion.c_ref = f32[4,27,8]{2,1,0:T(8,128)} fusion(f32[4,27,1,8]{3,2,1,0:T(1,128)S(1)} %slice.24, f32[4,27,7]{2,1,0:T(8,128)S(1)} %bitcast.21), kind=kLoop, calls=%fused_computation.14 | loop fusion | flops 864 | bytes 9936 | tf_op jit(solution)/shard_map/add | solution.py:269
  56.0 9.6 %shard_map.69 = f32[27,8]{1,0:T(8,128)} custom-call(f32[4,27,8]{2,1,0:T(8,128)} %fusion.c_ref), custom_call_target="tpu_custom_call" | custom-call | tf_op jit(solution)/shard_map/pallas_call | solution.py:332
  65.6 1.4 %copy.22 = f32[27,1,1,8]{0,3,2,1:T(8,128)} copy(f32[27,1,1,8]{3,0,2,1:T(8,128)} %bitcast.22) | data formatting | bytes 1728
  (6 shorter events, 0.1 us)
Async XLA Ops:
  0.6 19.9 %copy-start = (f32[8,16,16,128]{3,2,1,0:T(8,128)S(1)}, f32[8,16,16,128]{3,2,1,0:T(8,128)}, u32[]{:S(2)}) copy-start(f32[8,16,16,128]{3,2,1,0:T(8,128)} %param.5) | copy-start | bytes 3145732
  4.3 11.3 %collective-permute-start = (f32[10,4,16,128]{3,2,1,0:T(8,128)S(1)}, f32[10,4,16,128]{3,2,1,0:T(8,128)S(1)}, u32[]{:S(2)}, u32[]{:S(2)}) collective-permute-start(f32[10,4,16,128]{3,2,1,0:T(8,128)S(1)} %get-tuple-element.16), channel_id=1, source_target_pairs={{0,32},{32,64},{64,96},{96,128},{128,160},{160,192},{192,224},{1,3... | collective-permute-start | bytes 983048 | tf_op jit(solution)/shard_map/ppermute | solution.py:24
  8.1 12.5 %collective-permute-start.1 = (f32[10,4,16,128]{3,2,1,0:T(8,128)S(1)}, f32[10,4,16,128]{3,2,1,0:T(8,128)S(1)}, u32[]{:S(2)}, u32[]{:S(2)}) collective-permute-start(f32[10,4,16,128]{3,2,1,0:T(8,128)S(1)} %get-tuple-element.17), channel_id=1, source_target_pairs={{32,0},{64,32},{96,64},{128,96},{160,128},{192,160},{224,192},{33,... | collective-permute-start | bytes 983048 | tf_op jit(solution)/shard_map/ppermute | solution.py:27
  20.8 12.3 %collective-permute-start.2 = (f32[10,24,4,128]{3,2,1,0:T(4,128)S(1)}, f32[10,24,4,128]{3,2,1,0:T(4,128)S(1)}, u32[]{:S(2)}, u32[]{:S(2)}) collective-permute-start(f32[10,24,4,128]{3,2,1,0:T(4,128)S(1)} %get-tuple-element.14), channel_id=1, source_target_pairs={{0,1},{1,2},{2,3},{3,4},{4,5},{5,6},{6,7},{7,8},{8,9},{9,10},{10,1... | collective-permute-start | bytes 1474568 | tf_op jit(solution)/shard_map/ppermute | solution.py:24
  22.7 12.1 %collective-permute-start.3 = (f32[10,24,4,128]{3,2,1,0:T(4,128)S(1)}, f32[10,24,4,128]{3,2,1,0:T(4,128)S(1)}, u32[]{:S(2)}, u32[]{:S(2)}) collective-permute-start(f32[10,24,4,128]{3,2,1,0:T(4,128)S(1)} %get-tuple-element.15), channel_id=1, source_target_pairs={{1,0},{2,1},{3,2},{4,3},{5,4},{6,5},{7,6},{8,7},{9,8},{10,9},{11,1... | collective-permute-start | bytes 1474568 | tf_op jit(solution)/shard_map/ppermute | solution.py:27
  36.9 17.9 %copy-start.1 = (f32[216,64]{1,0:T(8,128)S(1)}, f32[216,64]{1,0:T(8,128)}, u32[]{:S(2)}) copy-start(f32[216,64]{1,0:T(8,128)} %constant.69.clone) | copy-start | bytes 165892

commit v2 on v1

--- a/solution.py
+++ b/solution.py
@@ -67,10 +67,98 @@
     return bits
 
 
-def smooth_kernel(ext_ref, basis_ref, prod_ref, tt, aux, valid, wa, wb, img):
-    _, XE, YE, L = ext_ref.shape
+def halo_window(ref, xs, ys):
+    if len(ref.shape) == 4:
+        return ref.at[:, xs, ys, :]
+    return ref.at[xs, ys, :]
+
+
+def halo_range(d, count, halo):
+    if d > 0:
+        return pl.ds(count - halo, halo), pl.ds(0, halo)
+    if d < 0:
+        return pl.ds(0, halo), pl.ds(halo + count, halo)
+    return pl.ds(0, count), pl.ds(halo, count)
+
+
+def smooth_kernel(
+    nx, ny,
+    basis_in, labels_in, class_perm, support_in, basis_ref, prod_ref,
+    eb, el, es, pm, tt, aux, valid, wa, wb, img, send_sem, recv_sem, local_sem,
+):
+    gi = lax.axis_index("gx")
+    gj = lax.axis_index("gy")
+    _, XE, YE, L = eb.shape
     NXL = basis_ref.shape[1]
     NYL = basis_ref.shape[2]
+    mesh_id = pl.DeviceIdType.MESH
+    sources = (basis_in, labels_in, support_in)
+    targets = (eb, el, es)
+    local_copies = []
+    for a in range(3):
+        local_copy = pltpu.make_async_copy(
+            sources[a], halo_window(targets[a], pl.ds(HX, NXL), pl.ds(HY, NYL)), local_sem.at[a]
+        )
+        local_copy.start()
+        local_copies.append(local_copy)
+
+    directions = [(dx, dy) for dx in (-1, 0, 1) for dy in (-1, 0, 1) if (dx, dy) != (0, 0)]
+
+    def has_device(x, y):
+        return (x >= 0) & (x < nx) & (y >= 0) & (y < ny)
+
+    peers = jnp.int32(0)
+    for dx, dy in directions:
+        _, to_x = halo_range(dx, NXL, HX)
+        _, to_y = halo_range(dy, NYL, HY)
+        from_here = has_device(gi - dx, gj - dy)
+        peers = peers + from_here.astype(jnp.int32)
+
+        @pl.when(jnp.logical_not(from_here))
+        def _():
+            for a in range(3):
+                window = halo_window(targets[a], to_x, to_y)
+                window[...] = jnp.zeros(window.shape, window.dtype)
+
+    barrier = pltpu.get_barrier_semaphore()
+    for dx, dy in directions:
+        @pl.when(has_device(gi + dx, gj + dy))
+        def _():
+            pl.semaphore_signal(barrier, 1, device_id=(gi + dx, gj + dy), device_id_type=mesh_id)
+
+    pl.semaphore_wait(barrier, peers)
+
+    def remote_copy(k, a, dx, dy, target_x, target_y):
+        from_x, to_x = halo_range(dx, NXL, HX)
+        from_y, to_y = halo_range(dy, NYL, HY)
+        return pltpu.make_async_remote_copy(
+            src_ref=halo_window(sources[a], from_x, from_y),
+            dst_ref=halo_window(targets[a], to_x, to_y),
+            send_sem=send_sem.at[3 * k + a],
+            recv_sem=recv_sem.at[3 * k + a],
+            device_id=(target_x, target_y),
+            device_id_type=mesh_id,
+        )
+
+    for k, (dx, dy) in enumerate(directions):
+        @pl.when(has_device(gi + dx, gj + dy))
+        def _():
+            for a in range(3):
+                remote_copy(k, a, dx, dy, gi + dx, gj + dy).start()
+
+    for local_copy in local_copies:
+        local_copy.wait()
+    for k, (dx, dy) in enumerate(directions):
+        @pl.when(has_device(gi + dx, gj + dy))
+        def _():
+            for a in range(3):
+                remote_copy(k, a, dx, dy, gi + dx, gj + dy).wait_send()
+
+        @pl.when(has_device(gi - dx, gj - dy))
+        def _():
+            for a in range(3):
+                remote_copy(k, a, dx, dy, gi - dx, gj - dy).wait_recv()
+
     row = lax.broadcasted_iota(jnp.int32, (YE, L), 0)
     lane = lax.broadcasted_iota(jnp.int32, (YE, L), 1)
     ry = (row + (CB - HY)) & (CB - 1)
@@ -80,14 +168,30 @@
     m_zhi = rz == CB - 1
     m_zlo = rz == 0
     m_rows = (row >= HY) & (row < HY + NYL)
+    global_y = gj * NYL + row - HY
+    inside_y = (global_y >= 0) & (global_y < ny * NYL)
+    node_y = gj + ((row + (CB - HY)) >> 4) < ny
+    node_z = (lane >> 4) + 1 < L // CB
+
+    def lookup(x, carry):
+        labels = el[x]
+        perm = jnp.zeros((YE, L), jnp.float32)
+        for c in range(class_perm.shape[0]):
+            perm = jnp.where(labels == c, class_perm[c], perm)
+        global_x = gi * NXL + x - HX
+        inside = inside_y & (global_x >= 0) & (global_x < nx * NXL)
+        pm[x] = jnp.where(inside, perm, 0.0)
+        return carry
+
+    lax.fori_loop(0, XE, lookup, 0)
 
     def xplace(x):
         return (x + (CB - HX)) & (CB - 1)
 
     def pre(x, carry):
-        pc = ext_ref[8, x]
-        pxp = jnp.where(x + 1 < XE, ext_ref[8, jnp.minimum(x + 1, XE - 1)], 0.0)
-        pxm = jnp.where(x >= 1, ext_ref[8, jnp.maximum(x - 1, 0)], 0.0)
+        pc = pm[x]
+        pxp = jnp.where(x + 1 < XE, pm[jnp.minimum(x + 1, XE - 1)], 0.0)
+        pxm = jnp.where(x >= 1, pm[jnp.maximum(x - 1, 0)], 0.0)
         pyp = pltpu.roll(pc, YE - 1, 0)
         pym = pltpu.roll(pc, 1, 0)
         pzp = pltpu.roll(pc, L - 1, 1)
@@ -115,11 +219,20 @@
         tt[9, x] = jnp.where(m_zhi, 0.0, t_zp)
         tt[10, x] = t_zm
         tt[11, x] = jnp.where(m_zlo, 0.0, t_zm)
-        sup = ext_ref[9, x].astype(jnp.int32)
+        sup = es[x]
+        node_x = gi + ((x + (CB - HX)) >> 4) < nx
         for s in range(8):
-            v = ((sup >> s) & 1).astype(jnp.float32)
+            bx, by, bz = corner_of(s)
+            keep = ((sup >> s) & 1) > 0
+            if bx:
+                keep = keep & node_x
+            if by:
+                keep = keep & node_y
+            if bz:
+                keep = keep & node_z
+            v = jnp.where(keep, 1.0, 0.0)
             valid[s, x] = v
-            wa[s, x] = ext_ref[s, x] * v
+            wa[s, x] = eb[s, x] * v
         return carry
 
     lax.fori_loop(0, XE, pre, 0)
@@ -229,39 +342,36 @@
     size_x, size_y, size_z = labels.shape
     assert size_x == CB and size_y == CB and size_z % CB == 0
     blocks_z = size_z // CB
-    permeability = class_lookup(labels, class_perm)
-    keep = existing_bits(
-        size_x,
-        size_y,
-        size_z,
-        lax.axis_index("gx") * size_x,
-        lax.axis_index("gy") * size_y,
-        lax.axis_size("gx") * size_x // CB,
-        lax.axis_size("gy") * size_y // CB,
-        blocks_z,
-    )
-    support_f = (support & keep).astype(jnp.float32)
-    packed = jnp.concatenate([initial_basis, permeability[None], support_f[None]], axis=0)
-    ext = with_halo(packed, (("gx", 1), ("gy", 2)), HX)
+    nx = lax.axis_size("gx")
+    ny = lax.axis_size("gy")
     XE, YE = size_x + 2 * HX, size_y + 2 * HY
     f32 = jnp.float32
+    vmem = pl.BlockSpec(memory_space=pltpu.VMEM)
     basis, prods = pl.pallas_call(
-        smooth_kernel,
+        functools.partial(smooth_kernel, nx, ny),
         out_shape=(
             jax.ShapeDtypeStruct((8, size_x, size_y, size_z), f32),
             jax.ShapeDtypeStruct((64, size_z), f32),
         ),
-        in_specs=[pl.BlockSpec(memory_space=pltpu.VMEM)],
-        out_specs=(pl.BlockSpec(memory_space=pltpu.VMEM), pl.BlockSpec(memory_space=pltpu.VMEM)),
+        in_specs=[vmem, vmem, pl.BlockSpec(memory_space=pltpu.SMEM), vmem],
+        out_specs=(vmem, vmem),
         scratch_shapes=[
+            pltpu.VMEM((8, XE, YE, size_z), f32),
+            pltpu.VMEM((XE, YE, size_z), jnp.int32),
+            pltpu.VMEM((XE, YE, size_z), jnp.int32),
+            pltpu.VMEM((XE, YE, size_z), f32),
             pltpu.VMEM((12, XE, YE, size_z), f32),
             pltpu.VMEM((2, XE, YE, size_z), f32),
             pltpu.VMEM((8, XE, YE, size_z), f32),
             pltpu.VMEM((8, XE, YE, size_z), f32),
             pltpu.VMEM((8, XE, YE, size_z), f32),
             pltpu.VMEM((8, size_x, YE, size_z), f32),
+            pltpu.SemaphoreType.DMA((24,)),
+            pltpu.SemaphoreType.DMA((24,)),
+            pltpu.SemaphoreType.DMA((3,)),
         ],
-    )(ext)
+        compiler_params=pltpu.CompilerParams(collective_id=1, has_side_effects=True),
+    )(initial_basis, labels, class_perm, support)
     block_sums = prods.reshape(64, blocks_z, CB).sum(axis=-1)
     placed = jnp.dot(
         jnp.asarray(assembly_matrix()), block_sums, precision=lax.Precision.HIGHEST

time: 67.4 us -> 52.4 us (0.78)
  Pallas kernels: 26.6 us -> 45.1 us
  waiting for transfers between devices: 16.8 us -> 0 us
  starting transfers between devices: 13.5 us -> 0 us
  other arithmetic: 6.67 us -> 0.74 us
  local copies, waits for them, and re-layouts: 2.34 us -> 4.64 us
    pallas_call x1, Pallas kernels: 17 us -> 37.3 us  [shards(): pl.pallas_call(functools.partial(smooth_kernel, nx, ny), out_shape=(jax.S...]
    ppermute x4 -> x0, waiting for transfers between devices: 16.8 us -> none  [the longest x2 10.1 us: with_halo(): lax.ppermute(lax.slice_in_dim(block, block.shape[dim] - width, None, axis...]
    ppermute x4 -> x0, starting transfers between devices: 13.5 us -> none  [the longest x2 7.77 us: with_halo(): lax.ppermute(lax.slice_in_dim(block, 0, width, axis=dim), axis, backward)]
    unnamed x6 -> x5, local copies, waits for them, and re-layouts: 1.4 us -> 3.66 us
    concatenate x1 -> x0, other arithmetic: 2.11 us -> none  [with_halo(): block = jnp.concatenate([low, block, high], axis=dim)]
    pallas_call x1, Pallas kernels: 9.58 us -> 7.79 us  [exchange_coarse(): pl.pallas_call(functools.partial(coarse_kernel, nx, ny), out_shape=jax.Sh...]
    slice x2 -> x0, other arithmetic: 1.32 us -> none  [with_halo(): lax.slice_in_dim(block, block.shape[dim] - width, None, axis=dim)]
    reduce_sum x1 -> x0, other arithmetic: 1.27 us -> none  [class_lookup(): jnp.sum(jnp.where(hits, class_perm[:, None, None, None], 0.0), axis=0)]
  transfers between devices with their start and end apart: 4 -> 0, of which waited for: 4 -> 0; matrix products, arithmetic and copies ran while one was open for 0% -> 0% of each run, Pallas kernels for 0% -> 0%
where the time goes in v2:
time: 52.4 us; the launch traced here: 51.5 us
  Pallas kernels  45.1 us (86%)
  local copies, waits for them, and re-layouts  4.64 us (9%)
  other arithmetic  0.74 us (1%)
  between operations  0.71 us (1%)
    pallas_call x1, Pallas kernels, shards(): pl.pallas_call(functools.partial(smooth_kernel, nx, ny), out_shape=(jax.S...  37.3 us
    pallas_call x1, Pallas kernels, exchange_coarse(): pl.pallas_call(functools.partial(coarse_kernel, nx, ny), out_shape=jax.Sh...  7.79 us
    unnamed x5, local copies, waits for them, and re-layouts  3.66 us

profile of v2, /device:TPU:70, one launch (start us, length us, event | category | flops | bytes accessed | tf_op | source)
XLA Modules:
  0.0 51.5 jit_solution(14877965997865790651)
XLA Ops:
  0.6 37.3 %shard_map.68 = (f32[8,16,16,128]{3,2,1,0:T(8,128)}, f32[64,128]{1,0:T(8,128)}) custom-call(f32[8,16,16,128]{3,2,1,0:T(8,128)} %basis_in.1, s32[16,16,128]{2,1,0:T(8,128)} %labels_in.1, f32[16]{0:T(128)} %class_perm.1, s32[16,16,128]{2,1,0:T(8,128)} %support_in.1), custom_call_target="tpu_custom_call" | custom-call | tf_op jit(solution)/shard_map/pallas_call | solution.py:350
  38.0 0.0 copy-start
  38.0 0.9 %copy.13 = f32[64,128]{0,1:T(8,128)S(1)} copy(f32[64,128]{1,0:T(8,128)} %get-tuple-element.5) | data formatting | bytes 65536 | tf_op jit(solution)/shard_map/pallas_call | solution.py:350
  38.9 0.0 copy-done
  38.9 0.3 fusion.1
  39.2 0.1 slice.9
  39.4 0.7 %fusion.c_ref = f32[4,27,8]{2,1,0:T(8,128)} fusion(f32[4,27,1,8]{3,2,1,0:T(1,128)S(1)} %slice.8, f32[4,27,7]{2,1,0:T(8,128)S(1)} %bitcast.15), kind=kLoop, calls=%fused_computation.2 | loop fusion | flops 864 | bytes 9936 | tf_op jit(solution)/shard_map/add | solution.py:379
  40.1 7.8 %shard_map.69 = f32[27,8]{1,0:T(8,128)} custom-call(f32[4,27,8]{2,1,0:T(8,128)} %fusion.c_ref), custom_call_target="tpu_custom_call" | custom-call | tf_op jit(solution)/shard_map/pallas_call | solution.py:442
  47.9 1.4 %copy.17 = f32[27,1,1,8]{0,3,2,1:T(8,128)} copy(f32[27,1,1,8]{3,0,2,1:T(8,128)} %bitcast.16) | data formatting | bytes 1728
  49.3 2.3 %copy.27 = f32[8,16,16,128]{3,2,1,0:T(8,128)} copy(f32[8,16,16,128]{3,2,1,0:T(8,128)} %get-tuple-element.14) | data formatting | bytes 2097152
  (3 shorter events, 0.1 us)
Async XLA Ops:
  38.0 0.9 %copy-start = (f32[216,64]{1,0:T(8,128)S(1)}, f32[216,64]{1,0:T(8,128)}, u32[]{:S(2)}) copy-start(f32[216,64]{1,0:T(8,128)} %constant.6.clone) | copy-start | bytes 165892

commit v3 on v2

--- a/solution.py
+++ b/solution.py
@@ -79,6 +79,14 @@
     if d < 0:
         return pl.ds(0, halo), pl.ds(halo + count, halo)
     return pl.ds(0, count), pl.ds(halo, count)
+
+
+def halo_rows(d, count, halo):
+    if d > 0:
+        return pl.ds(count - halo, halo), pl.ds(count + halo, halo)
+    if d < 0:
+        return pl.ds(0, halo), pl.ds(count, halo)
+    return pl.ds(0, count), pl.ds(0, count)
 
 
 def smooth_kernel(
@@ -97,7 +105,7 @@
     local_copies = []
     for a in range(3):
         local_copy = pltpu.make_async_copy(
-            sources[a], halo_window(targets[a], pl.ds(HX, NXL), pl.ds(HY, NYL)), local_sem.at[a]
+            sources[a], halo_window(targets[a], pl.ds(HX, NXL), pl.ds(0, NYL)), local_sem.at[a]
         )
         local_copy.start()
         local_copies.append(local_copy)
@@ -110,7 +118,7 @@
     peers = jnp.int32(0)
     for dx, dy in directions:
         _, to_x = halo_range(dx, NXL, HX)
-        _, to_y = halo_range(dy, NYL, HY)
+        _, to_y = halo_rows(dy, NYL, HY)
         from_here = has_device(gi - dx, gj - dy)
         peers = peers + from_here.astype(jnp.int32)
 
@@ -130,7 +138,7 @@
 
     def remote_copy(k, a, dx, dy, target_x, target_y):
         from_x, to_x = halo_range(dx, NXL, HX)
-        from_y, to_y = halo_range(dy, NYL, HY)
+        from_y, to_y = halo_rows(dy, NYL, HY)
         return pltpu.make_async_remote_copy(
             src_ref=halo_window(sources[a], from_x, from_y),
             dst_ref=halo_window(targets[a], to_x, to_y),
@@ -161,16 +169,16 @@
 
     row = lax.broadcasted_iota(jnp.int32, (YE, L), 0)
     lane = lax.broadcasted_iota(jnp.int32, (YE, L), 1)
-    ry = (row + (CB - HY)) & (CB - 1)
-    m_yhi = ry == CB - 1
-    m_ylo = ry == 0
+    m_yhi = (row == NYL - 1) | (row == YE - 1)
+    m_ylo = (row == 0) | (row == NYL)
     rz = lane & (CB - 1)
     m_zhi = rz == CB - 1
     m_zlo = rz == 0
-    m_rows = (row >= HY) & (row < HY + NYL)
-    global_y = gj * NYL + row - HY
+    m_rows = row < NYL
+    block_y = gj + jnp.where(row < NYL, 0, jnp.where(row < NYL + HY, 1, -1))
+    global_y = jnp.where(row < NYL + HY, gj * NYL + row, gj * NYL + row - YE)
     inside_y = (global_y >= 0) & (global_y < ny * NYL)
-    node_y = gj + ((row + (CB - HY)) >> 4) < ny
+    node_y = block_y + 1 < ny
     node_z = (lane >> 4) + 1 < L // CB
 
     def lookup(x, carry):
@@ -309,7 +317,7 @@
             c = basis_buf[s, x]
             inflow = inflow_of(basis_buf, x, s, c)
             img[s, x - HX] = jnp.where(m_rows, diag * c - inflow, 0.0)
-            basis_ref[s, x - HX] = c[HY:HY + NYL, :]
+            basis_ref[s, x - HX] = c[:NYL, :]
         return carry
 
     lax.fori_loop(HX, HX + NXL, image, 0)

time: 52.4 us -> 52.1 us (level)
  no operation moved by 1% of the time
where the time goes in v3:
time: 52.1 us; the launch traced here: 51.3 us
  Pallas kernels  44.9 us (86%)
  local copies, waits for them, and re-layouts  4.64 us (9%)
  other arithmetic  0.74 us (1%)
  between operations  0.71 us (1%)
    pallas_call x1, Pallas kernels, shards(): pl.pallas_call(functools.partial(smooth_kernel, nx, ny), out_shape=(jax.S...  37.1 us
    pallas_call x1, Pallas kernels, exchange_coarse(): pl.pallas_call(functools.partial(coarse_kernel, nx, ny), out_shape=jax.Sh...  7.79 us
    unnamed x5, local copies, waits for them, and re-layouts  3.66 us

profile of v3, /device:TPU:70, one launch (start us, length us, event | category | flops | bytes accessed | tf_op | source)
XLA Modules:
  0.0 51.3 jit_solution(10147436394394628452)
XLA Ops:
  0.6 37.1 %shard_map.68 = (f32[8,16,16,128]{3,2,1,0:T(8,128)}, f32[64,128]{1,0:T(8,128)}) custom-call(f32[8,16,16,128]{3,2,1,0:T(8,128)} %basis_in.1, s32[16,16,128]{2,1,0:T(8,128)} %labels_in.1, f32[16]{0:T(128)} %class_perm.1, s32[16,16,128]{2,1,0:T(8,128)} %support_in.1), custom_call_target="tpu_custom_call" | custom-call | tf_op jit(solution)/shard_map/pallas_call | solution.py:358
  37.7 0.0 copy-start
  37.7 0.9 %copy.13 = f32[64,128]{0,1:T(8,128)S(1)} copy(f32[64,128]{1,0:T(8,128)} %get-tuple-element.5) | data formatting | bytes 65536 | tf_op jit(solution)/shard_map/pallas_call | solution.py:358
  38.6 0.0 copy-done
  38.7 0.3 fusion.1
  39.0 0.1 slice.9
  39.1 0.7 %fusion.c_ref = f32[4,27,8]{2,1,0:T(8,128)} fusion(f32[4,27,1,8]{3,2,1,0:T(1,128)S(1)} %slice.8, f32[4,27,7]{2,1,0:T(8,128)S(1)} %bitcast.15), kind=kLoop, calls=%fused_computation.2 | loop fusion | flops 864 | bytes 9936 | tf_op jit(solution)/shard_map/add | solution.py:387
  39.8 7.8 %shard_map.69 = f32[27,8]{1,0:T(8,128)} custom-call(f32[4,27,8]{2,1,0:T(8,128)} %fusion.c_ref), custom_call_target="tpu_custom_call" | custom-call | tf_op jit(solution)/shard_map/pallas_call | solution.py:450
  47.6 1.4 %copy.17 = f32[27,1,1,8]{0,3,2,1:T(8,128)} copy(f32[27,1,1,8]{3,0,2,1:T(8,128)} %bitcast.16) | data formatting | bytes 1728
  49.0 2.3 %copy.27 = f32[8,16,16,128]{3,2,1,0:T(8,128)} copy(f32[8,16,16,128]{3,2,1,0:T(8,128)} %get-tuple-element.14) | data formatting | bytes 2097152
  (3 shorter events, 0.1 us)
Async XLA Ops:
  37.7 0.9 %copy-start = (f32[216,64]{1,0:T(8,128)S(1)}, f32[216,64]{1,0:T(8,128)}, u32[]{:S(2)}) copy-start(f32[216,64]{1,0:T(8,128)} %constant.6.clone) | copy-start | bytes 165892

commit v4 on v3

--- a/solution.py
+++ b/solution.py
@@ -91,8 +91,9 @@
 
 def smooth_kernel(
     nx, ny,
-    basis_in, labels_in, class_perm, support_in, basis_ref, prod_ref,
-    eb, el, es, pm, tt, aux, valid, wa, wb, img, send_sem, recv_sem, local_sem,
+    basis_in, labels_in, class_perm, support_in, placing, basis_ref, coarse_ref,
+    eb, el, es, pm, tt, aux, valid, wa, wb, img, prod_ref, terms, received,
+    send_sem, recv_sem, local_sem, coarse_send, coarse_recv,
 ):
     gi = lax.axis_index("gx")
     gj = lax.axis_index("gy")
@@ -127,6 +128,12 @@
             for a in range(3):
                 window = halo_window(targets[a], to_x, to_y)
                 window[...] = jnp.zeros(window.shape, window.dtype)
+
+    coarse_routes = ((2, 1, 0), (1, 0, 1), (3, 1, 1))
+    for k, (_, dx, dy) in enumerate(coarse_routes):
+        @pl.when(jnp.logical_not(has_device(gi - dx, gj - dy)))
+        def _():
+            received[k] = jnp.zeros(received.shape[1:], received.dtype)
 
     barrier = pltpu.get_barrier_semaphore()
     for dx, dy in directions:
@@ -333,16 +340,59 @@
         for s2 in range(8):
             prod_ref[pl.ds(s1 * 8 + s2, 1), :] = jnp.sum(acc[s2], axis=0, keepdims=True)
 
-
-def assembly_matrix():
-    table = np.zeros((4 * 27 * 2, 64), np.float32)
+    nbz = L // CB
+    node = lax.broadcasted_iota(jnp.int32, (nbz, L), 0)
+    block = lax.broadcasted_iota(jnp.int32, (nbz, L), 1) >> 4
+    same_node = jnp.where(block == node, 1.0, 0.0)
+    node_above = jnp.where(block + 1 == node, 1.0, 0.0)
+    pairs = prod_ref[...]
+    along_lanes = (((1,), (1,)), ((), ()))
+    exact = lax.Precision.HIGHEST
+    low = lax.dot_general(same_node, pairs, along_lanes, precision=exact,
+                          preferred_element_type=jnp.float32)
+    high = lax.dot_general(node_above, pairs, along_lanes, precision=exact,
+                           preferred_element_type=jnp.float32)
+    for c in range(4):
+        terms[c] = jnp.dot(low, placing[c, 0], precision=exact,
+                           preferred_element_type=jnp.float32) + jnp.dot(
+            high, placing[c, 1], precision=exact, preferred_element_type=jnp.float32)
+
+    def coarse_copy(k, c, target_x, target_y):
+        return pltpu.make_async_remote_copy(
+            src_ref=terms.at[c],
+            dst_ref=received.at[k],
+            send_sem=coarse_send.at[k],
+            recv_sem=coarse_recv.at[k],
+            device_id=(target_x, target_y),
+            device_id_type=mesh_id,
+        )
+
+    for k, (c, dx, dy) in enumerate(coarse_routes):
+        @pl.when(has_device(gi + dx, gj + dy))
+        def _():
+            coarse_copy(k, c, gi + dx, gj + dy).start()
+
+    for k, (c, dx, dy) in enumerate(coarse_routes):
+        @pl.when(has_device(gi + dx, gj + dy))
+        def _():
+            coarse_copy(k, c, gi + dx, gj + dy).wait_send()
+
+        @pl.when(has_device(gi - dx, gj - dy))
+        def _():
+            coarse_copy(k, c, gi - dx, gj - dy).wait_recv()
+
+    total = terms[0] + received[0] + received[1] + received[2]
+    coarse_ref[...] = total[:, : coarse_ref.shape[1]]
+
+
+def placing_matrix():
+    table = np.zeros((4, 2, 64, 32), np.float32)
     for first_slot in range(8):
         for second_slot in range(8):
             one_x, one_y, one_z = corner_of(first_slot)
             two_x, two_y, two_z = corner_of(second_slot)
             offset_index = 9 * (two_x - one_x + 1) + 3 * (two_y - one_y + 1) + (two_z - one_z + 1)
-            row = ((one_x * 2 + one_y) * 27 + offset_index) * 2 + one_z
-            table[row, first_slot * 8 + second_slot] = 1.0
+            table[one_x * 2 + one_y, one_z, first_slot * 8 + second_slot, offset_index] = 1.0
     return table
 
 
@@ -355,13 +405,14 @@
     XE, YE = size_x + 2 * HX, size_y + 2 * HY
     f32 = jnp.float32
     vmem = pl.BlockSpec(memory_space=pltpu.VMEM)
-    basis, prods = pl.pallas_call(
+    blocks_z = size_z // CB
+    basis, coarse = pl.pallas_call(
         functools.partial(smooth_kernel, nx, ny),
         out_shape=(
             jax.ShapeDtypeStruct((8, size_x, size_y, size_z), f32),
-            jax.ShapeDtypeStruct((64, size_z), f32),
+            jax.ShapeDtypeStruct((blocks_z, 27), f32),
         ),
-        in_specs=[vmem, vmem, pl.BlockSpec(memory_space=pltpu.SMEM), vmem],
+        in_specs=[vmem, vmem, pl.BlockSpec(memory_space=pltpu.SMEM), vmem, vmem],
         out_specs=(vmem, vmem),
         scratch_shapes=[
             pltpu.VMEM((8, XE, YE, size_z), f32),
@@ -374,91 +425,18 @@
             pltpu.VMEM((8, XE, YE, size_z), f32),
             pltpu.VMEM((8, XE, YE, size_z), f32),
             pltpu.VMEM((8, size_x, YE, size_z), f32),
+            pltpu.VMEM((64, size_z), f32),
+            pltpu.VMEM((4, blocks_z, 32), f32),
+            pltpu.VMEM((3, blocks_z, 32), f32),
             pltpu.SemaphoreType.DMA((24,)),
             pltpu.SemaphoreType.DMA((24,)),
             pltpu.SemaphoreType.DMA((3,)),
-        ],
-        compiler_params=pltpu.CompilerParams(collective_id=1, has_side_effects=True),
-    )(initial_basis, labels, class_perm, support)
-    block_sums = prods.reshape(64, blocks_z, CB).sum(axis=-1)
-    placed = jnp.dot(
-        jnp.asarray(assembly_matrix()), block_sums, precision=lax.Precision.HIGHEST
-    ).reshape(4, 27, 2, blocks_z)
-    contrib = placed[:, :, 0] + jnp.pad(placed[:, :, 1, :-1], ((0, 0), (0, 0), (1, 0)))
-    owned = exchange_coarse(contrib, lax.axis_size("gx"), lax.axis_size("gy"))
-    return (basis, owned.reshape(27, 1, 1, blocks_z))
-
-
-def coarse_kernel(nx, ny, c_ref, o_ref, recv, send_sem, recv_sem):
-    i = lax.axis_index("gx")
-    j = lax.axis_index("gy")
-    mesh_id = pl.DeviceIdType.MESH
-    recv[...] = jnp.zeros_like(recv)
-    routes = ((2, 0, 1, 0), (1, 1, 0, 1), (3, 2, 1, 1))
-    barrier = pltpu.get_barrier_semaphore()
-    for _, _, dx, dy in routes:
-        has_dst = (i + dx < nx) & (j + dy < ny)
-        has_src = (i - dx >= 0) & (j - dy >= 0)
-
-        @pl.when(has_dst)
-        def _():
-            pl.semaphore_signal(barrier, 1, device_id=(i + dx, j + dy), device_id_type=mesh_id)
-
-        @pl.when(has_src)
-        def _():
-            pl.semaphore_signal(barrier, 1, device_id=(i - dx, j - dy), device_id_type=mesh_id)
-
-    peers = jnp.int32(0)
-    for _, _, dx, dy in routes:
-        has_dst = (i + dx < nx) & (j + dy < ny)
-        has_src = (i - dx >= 0) & (j - dy >= 0)
-        peers = peers + has_dst.astype(jnp.int32) + has_src.astype(jnp.int32)
-    pl.semaphore_wait(barrier, peers)
-
-    copies = []
-    for slot, k, dx, dy in routes:
-        has_dst = (i + dx < nx) & (j + dy < ny)
-        has_src = (i - dx >= 0) & (j - dy >= 0)
-        out_copy = pltpu.make_async_remote_copy(
-            src_ref=c_ref.at[slot],
-            dst_ref=recv.at[k],
-            send_sem=send_sem.at[k],
-            recv_sem=recv_sem.at[k],
-            device_id=(jnp.minimum(i + dx, nx - 1), jnp.minimum(j + dy, ny - 1)),
-            device_id_type=mesh_id,
-        )
-        copies.append((out_copy, has_dst, has_src))
-
-        @pl.when(has_dst)
-        def _():
-            out_copy.start()
-
-    for out_copy, has_dst, has_src in copies:
-        @pl.when(has_dst)
-        def _():
-            out_copy.wait_send()
-
-        @pl.when(has_src)
-        def _():
-            out_copy.wait_recv()
-
-    o_ref[...] = c_ref[0] + recv[0] + recv[1] + recv[2]
-
-
-def exchange_coarse(contrib, nx, ny):
-    _, rows, cols = contrib.shape
-    return pl.pallas_call(
-        functools.partial(coarse_kernel, nx, ny),
-        out_shape=jax.ShapeDtypeStruct((rows, cols), jnp.float32),
-        in_specs=[pl.BlockSpec(memory_space=pltpu.VMEM)],
-        out_specs=pl.BlockSpec(memory_space=pltpu.VMEM),
-        scratch_shapes=[
-            pltpu.VMEM((3, rows, cols), jnp.float32),
             pltpu.SemaphoreType.DMA((3,)),
             pltpu.SemaphoreType.DMA((3,)),
         ],
-        compiler_params=pltpu.CompilerParams(collective_id=0, has_side_effects=True),
-    )(contrib)
+        compiler_params=pltpu.CompilerParams(collective_id=1, has_side_effects=True),
+    )(initial_basis, labels, class_perm, support, jnp.asarray(placing_matrix()))
+    return (basis, coarse.T.reshape(27, 1, 1, blocks_z))
 
 
 def solution(mesh):

time: 52.1 us -> 43.7 us (0.84)
  Pallas kernels: 44.9 us -> 39.7 us
  local copies, waits for them, and re-layouts: 4.64 us -> 2.87 us
  other arithmetic: 0.74 us -> 0 us
    pallas_call x1 -> x0, Pallas kernels: 7.79 us -> none  [exchange_coarse(): pl.pallas_call(functools.partial(coarse_kernel, nx, ny), out_shape=jax.Sh...]
    pallas_call x1, Pallas kernels: 37.1 us -> 39.7 us  [shards(): pl.pallas_call(functools.partial(smooth_kernel, nx, ny), out_shape=(jax.S...]
    pallas_call x1 -> x0, local copies, waits for them, and re-layouts: 0.88 us -> none  [shards(): pl.pallas_call(functools.partial(smooth_kernel, nx, ny), out_shape=(jax.S...]
    unnamed x5 -> x4, local copies, waits for them, and re-layouts: 3.66 us -> 2.87 us
    add x1 -> x0, other arithmetic: 0.72 us -> none  [shards(): placed[:, :, 0] + jnp.pad(placed[:, :, 1, :-1], ((0, 0), (0, 0), (1, 0)))]
where the time goes in v4:
time: 43.7 us; the launch traced here: 43.2 us
  Pallas kernels  39.7 us (91%)
  local copies, waits for them, and re-layouts  2.87 us (7%)
  between operations  0.65 us (1%)
    pallas_call x1, Pallas kernels, shards(): pl.pallas_call(functools.partial(smooth_kernel, nx, ny), out_shape=(jax.S...  39.7 us
    unnamed x4, local copies, waits for them, and re-layouts  2.87 us

profile of v4, /device:TPU:70, one launch (start us, length us, event | category | flops | bytes accessed | tf_op | source)
XLA Modules:
  0.0 43.2 jit_solution(2748875195214119599)
XLA Ops:
  0.6 39.7 %shard_map.68 = (f32[8,16,16,128]{3,2,1,0:T(8,128)}, f32[8,27]{1,0:T(8,128)}) custom-call(f32[8,16,16,128]{3,2,1,0:T(8,128)} %basis_in.1, s32[16,16,128]{2,1,0:T(8,128)} %labels_in.1, f32[16]{0:T(128)} %class_perm.1, s32[16,16,128]{2,1,0:T(8,128)} %support_in.1, f32[4,2,64,32]{3,2,1,0:T(8,128)} %constant.2.clone.placing), custom_call_target="tpu_custom_call" | custom-call | tf_op jit(solution)/shard_map/pallas_call | solution.py:409
  40.3 0.0 copy-start
  40.3 2.3 %copy.9 = f32[8,16,16,128]{3,2,1,0:T(8,128)} copy(f32[8,16,16,128]{3,2,1,0:T(8,128)} %get-tuple-element.8) | data formatting | bytes 2097152
  42.6 0.0 copy-done
  42.6 0.6 %copy.10 = f32[27,1,1,8]{0,3,2,1:T(8,128)} copy(f32[27,1,1,8]{0,3,2,1:T(8,128)S(1)} %bitcast.3) | data formatting | bytes 1728
Async XLA Ops:
  40.3 2.3 %copy-start = (f32[8,27]{1,0:T(8,128)S(1)}, f32[8,27]{1,0:T(8,128)}, u32[]{:S(2)}) copy-start(f32[8,27]{1,0:T(8,128)} %get-tuple-element.5) | copy-start | bytes 2596

commit v5 on v4

--- a/solution.py
+++ b/solution.py
@@ -9,8 +9,8 @@
 
 CB = 16
 ITERS = 3
-HX = ITERS + 1
-HY = ITERS + 1
+HX = ITERS
+HY = ITERS
 
 omega_jacobi = 2.0 / 3.0
 renorm_floor = 0.5
@@ -67,9 +67,9 @@
     return bits
 
 
-def halo_window(ref, xs, ys):
+def halo_window(ref, xs, ys, slots=None):
     if len(ref.shape) == 4:
-        return ref.at[:, xs, ys, :]
+        return ref.at[slots if slots is not None else slice(None), xs, ys, :]
     return ref.at[xs, ys, :]
 
 
@@ -81,19 +81,39 @@
     return pl.ds(0, count), pl.ds(halo, count)
 
 
-def halo_rows(d, count, halo):
+def halo_rows(d, count, halo, total):
     if d > 0:
-        return pl.ds(count - halo, halo), pl.ds(count + halo, halo)
+        return pl.ds(count - halo, halo), pl.ds(total - halo, halo)
     if d < 0:
         return pl.ds(0, halo), pl.ds(count, halo)
     return pl.ds(0, count), pl.ds(0, count)
 
 
+def slot_runs(slots):
+    runs = []
+    for s in sorted(slots):
+        if runs and runs[-1][1] == s:
+            runs[-1][1] = s + 1
+        else:
+            runs.append([s, s + 1])
+    return [pl.ds(lo, hi - lo) for lo, hi in runs]
+
+
+def shared_slots(dx, dy):
+    keep = []
+    for s in range(8):
+        bx, by, _ = corner_of(s)
+        if (dx > 0 and not bx) or (dx < 0 and bx) or (dy > 0 and not by) or (dy < 0 and by):
+            continue
+        keep.append(s)
+    return keep
+
+
 def smooth_kernel(
     nx, ny,
     basis_in, labels_in, class_perm, support_in, placing, basis_ref, coarse_ref,
-    eb, el, es, pm, tt, aux, valid, wa, wb, img, prod_ref, terms, received,
-    send_sem, recv_sem, local_sem, coarse_send, coarse_recv,
+    eb, el, es, pm, tt, aux, valid, wa, wb, wc, img, prod_ref, terms, received,
+    send_sem, recv_sem, local_sem, coarse_send, coarse_recv, edge_send, edge_recv,
 ):
     gi = lax.axis_index("gx")
     gj = lax.axis_index("gy")
@@ -116,12 +136,27 @@
     def has_device(x, y):
         return (x >= 0) & (x < nx) & (y >= 0) & (y < ny)
 
+    def pieces(dx, dy):
+        return [(0, run) for run in slot_runs(shared_slots(dx, dy))] + [(1, None), (2, None)]
+
+    def edge_pieces(dx, dy):
+        from_x = {1: pl.ds(HX + NXL - 1, 1), -1: pl.ds(HX, 1), 0: pl.ds(HX, NXL)}[dx]
+        to_x = {1: pl.ds(HX - 1, 1), -1: pl.ds(HX + NXL, 1), 0: pl.ds(HX, NXL)}[dx]
+        from_y = {1: pl.ds(NYL - 1, 1), -1: pl.ds(0, 1), 0: pl.ds(0, NYL)}[dy]
+        to_y = {1: pl.ds(YE - 1, 1), -1: pl.ds(NYL, 1), 0: pl.ds(0, NYL)}[dy]
+        return [(run, from_x, to_x, from_y, to_y) for run in slot_runs(shared_slots(dx, dy))]
+
+    faces = ((1, 0), (-1, 0), (0, 1), (0, -1))
     peers = jnp.int32(0)
     for dx, dy in directions:
         _, to_x = halo_range(dx, NXL, HX)
-        _, to_y = halo_rows(dy, NYL, HY)
+        _, to_y = halo_rows(dy, NYL, HY, YE)
         from_here = has_device(gi - dx, gj - dy)
         peers = peers + from_here.astype(jnp.int32)
+        unshared = [s for s in range(8) if s not in shared_slots(dx, dy)]
+        for run in slot_runs(unshared):
+            window = halo_window(eb, to_x, to_y, run)
+            window[...] = jnp.zeros(window.shape, window.dtype)
 
         @pl.when(jnp.logical_not(from_here))
         def _():
@@ -129,6 +164,20 @@
                 window = halo_window(targets[a], to_x, to_y)
                 window[...] = jnp.zeros(window.shape, window.dtype)
 
+    if NYL + HY < YE - HY:
+        junction = pl.ds(NYL + HY, YE - 2 * HY - NYL)
+        for a in range(3):
+            window = halo_window(targets[a], pl.ds(0, XE), junction)
+            window[...] = jnp.zeros(window.shape, window.dtype)
+    window = wc.at[:, pl.ds(HX, NXL), pl.ds(NYL, YE - NYL), :]
+    window[...] = jnp.zeros(window.shape, window.dtype)
+    for dx, dy in faces:
+        @pl.when(jnp.logical_not(has_device(gi - dx, gj - dy)))
+        def _():
+            for run, _, to_x, _, to_y in edge_pieces(dx, dy):
+                window = wc.at[run, to_x, to_y, :]
+                window[...] = jnp.zeros(window.shape, window.dtype)
+
     coarse_routes = ((2, 1, 0), (1, 0, 1), (3, 1, 1))
     for k, (_, dx, dy) in enumerate(coarse_routes):
         @pl.when(jnp.logical_not(has_device(gi - dx, gj - dy)))
@@ -143,14 +192,15 @@
 
     pl.semaphore_wait(barrier, peers)
 
-    def remote_copy(k, a, dx, dy, target_x, target_y):
+    def remote_copy(k, p, dx, dy, target_x, target_y):
         from_x, to_x = halo_range(dx, NXL, HX)
-        from_y, to_y = halo_rows(dy, NYL, HY)
+        from_y, to_y = halo_rows(dy, NYL, HY, YE)
+        a, run = pieces(dx, dy)[p]
         return pltpu.make_async_remote_copy(
-            src_ref=halo_window(sources[a], from_x, from_y),
-            dst_ref=halo_window(targets[a], to_x, to_y),
-            send_sem=send_sem.at[3 * k + a],
-            recv_sem=recv_sem.at[3 * k + a],
+            src_ref=halo_window(sources[a], from_x, from_y, run),
+            dst_ref=halo_window(targets[a], to_x, to_y, run),
+            send_sem=send_sem.at[4 * k + p],
+            recv_sem=recv_sem.at[4 * k + p],
             device_id=(target_x, target_y),
             device_id_type=mesh_id,
         )
@@ -158,21 +208,21 @@
     for k, (dx, dy) in enumerate(directions):
         @pl.when(has_device(gi + dx, gj + dy))
         def _():
-            for a in range(3):
-                remote_copy(k, a, dx, dy, gi + dx, gj + dy).start()
+            for p in range(len(pieces(dx, dy))):
+                remote_copy(k, p, dx, dy, gi + dx, gj + dy).start()
 
     for local_copy in local_copies:
         local_copy.wait()
     for k, (dx, dy) in enumerate(directions):
         @pl.when(has_device(gi + dx, gj + dy))
         def _():
-            for a in range(3):
-                remote_copy(k, a, dx, dy, gi + dx, gj + dy).wait_send()
+            for p in range(len(pieces(dx, dy))):
+                remote_copy(k, p, dx, dy, gi + dx, gj + dy).wait_send()
 
         @pl.when(has_device(gi - dx, gj - dy))
         def _():
-            for a in range(3):
-                remote_copy(k, a, dx, dy, gi - dx, gj - dy).wait_recv()
+            for p in range(len(pieces(dx, dy))):
+                remote_copy(k, p, dx, dy, gi - dx, gj - dy).wait_recv()
 
     row = lax.broadcasted_iota(jnp.int32, (YE, L), 0)
     lane = lax.broadcasted_iota(jnp.int32, (YE, L), 1)
@@ -182,8 +232,8 @@
     m_zhi = rz == CB - 1
     m_zlo = rz == 0
     m_rows = row < NYL
-    block_y = gj + jnp.where(row < NYL, 0, jnp.where(row < NYL + HY, 1, -1))
-    global_y = jnp.where(row < NYL + HY, gj * NYL + row, gj * NYL + row - YE)
+    block_y = gj + jnp.where(row < NYL, 0, jnp.where(row < YE - HY, 1, -1))
+    global_y = jnp.where(row < YE - HY, gj * NYL + row, gj * NYL + row - YE)
     inside_y = (global_y >= 0) & (global_y < ny * NYL)
     node_y = block_y + 1 < ny
     node_z = (lane >> 4) + 1 < L // CB
@@ -304,7 +354,7 @@
     for step in range(ITERS):
         sweep(bufs[step % 2], bufs[(step + 1) % 2], step + 1, XE - step - 1)
     last = bufs[ITERS % 2]
-    basis_buf = bufs[(ITERS + 1) % 2]
+    basis_buf = wc
 
     def normalize(x, carry):
         vals = [last[s, x] for s in range(8)]
@@ -313,10 +363,38 @@
             total = total + vals[s]
         scale = jnp.maximum(total, renorm_floor)
         for s in range(8):
-            basis_buf[s, x] = vals[s] / scale
+            basis_buf[s, x, pl.ds(0, NYL), :] = (vals[s] / scale)[:NYL, :]
         return carry
 
-    lax.fori_loop(ITERS, XE - ITERS, normalize, 0)
+    lax.fori_loop(HX, HX + NXL, normalize, 0)
+
+    def edge_copy(k, p, dx, dy, target_x, target_y):
+        run, from_x, to_x, from_y, to_y = edge_pieces(dx, dy)[p]
+        return pltpu.make_async_remote_copy(
+            src_ref=wc.at[run, from_x, from_y, :],
+            dst_ref=wc.at[run, to_x, to_y, :],
+            send_sem=edge_send.at[2 * k + p],
+            recv_sem=edge_recv.at[2 * k + p],
+            device_id=(target_x, target_y),
+            device_id_type=mesh_id,
+        )
+
+    for k, (dx, dy) in enumerate(faces):
+        @pl.when(has_device(gi + dx, gj + dy))
+        def _():
+            for p in range(len(edge_pieces(dx, dy))):
+                edge_copy(k, p, dx, dy, gi + dx, gj + dy).start()
+
+    for k, (dx, dy) in enumerate(faces):
+        @pl.when(has_device(gi + dx, gj + dy))
+        def _():
+            for p in range(len(edge_pieces(dx, dy))):
+                edge_copy(k, p, dx, dy, gi + dx, gj + dy).wait_send()
+
+        @pl.when(has_device(gi - dx, gj - dy))
+        def _():
+            for p in range(len(edge_pieces(dx, dy))):
+                edge_copy(k, p, dx, dy, gi - dx, gj - dy).wait_recv()
 
     def image(x, carry):
         diag = aux[0, x]
@@ -402,7 +480,8 @@
     blocks_z = size_z // CB
     nx = lax.axis_size("gx")
     ny = lax.axis_size("gy")
-    XE, YE = size_x + 2 * HX, size_y + 2 * HY
+    XE = size_x + 2 * HX
+    YE = -(-(size_y + 2 * HY) // 8) * 8
     f32 = jnp.float32
     vmem = pl.BlockSpec(memory_space=pltpu.VMEM)
     blocks_z = size_z // CB
@@ -424,15 +503,18 @@
             pltpu.VMEM((8, XE, YE, size_z), f32),
             pltpu.VMEM((8, XE, YE, size_z), f32),
             pltpu.VMEM((8, XE, YE, size_z), f32),
+            pltpu.VMEM((8, XE, YE, size_z), f32),
             pltpu.VMEM((8, size_x, YE, size_z), f32),
             pltpu.VMEM((64, size_z), f32),
             pltpu.VMEM((4, blocks_z, 32), f32),
             pltpu.VMEM((3, blocks_z, 32), f32),
-            pltpu.SemaphoreType.DMA((24,)),
-            pltpu.SemaphoreType.DMA((24,)),
+            pltpu.SemaphoreType.DMA((32,)),
+            pltpu.SemaphoreType.DMA((32,)),
             pltpu.SemaphoreType.DMA((3,)),
             pltpu.SemaphoreType.DMA((3,)),
             pltpu.SemaphoreType.DMA((3,)),
+            pltpu.SemaphoreType.DMA((8,)),
+            pltpu.SemaphoreType.DMA((8,)),
         ],
         compiler_params=pltpu.CompilerParams(collective_id=1, has_side_effects=True),
     )(initial_basis, labels, class_perm, support, jnp.asarray(placing_matrix()))

time: 43.7 us -> 41.1 us (0.941)
  Pallas kernels: 39.7 us -> 37.2 us
    pallas_call x1, Pallas kernels: 39.7 us -> 37.2 us  [shards(): pl.pallas_call(functools.partial(smooth_kernel, nx, ny), out_shape=(jax.S...]
where the time goes in v5:
time: 41.1 us; the launch traced here: 40.7 us
  Pallas kernels  37.2 us (91%)
  local copies, waits for them, and re-layouts  2.87 us (7%)
  between operations  0.65 us (2%)
    pallas_call x1, Pallas kernels, shards(): pl.pallas_call(functools.partial(smooth_kernel, nx, ny), out_shape=(jax.S...  37.2 us
    unnamed x4, local copies, waits for them, and re-layouts  2.87 us

profile of v5, /device:TPU:70, one launch (start us, length us, event | category | flops | bytes accessed | tf_op | source)
XLA Modules:
  0.0 40.7 jit_solution(617364197338624953)
XLA Ops:
  0.6 37.2 %shard_map.68 = (f32[8,16,16,128]{3,2,1,0:T(8,128)}, f32[8,27]{1,0:T(8,128)}) custom-call(f32[8,16,16,128]{3,2,1,0:T(8,128)} %basis_in.1, s32[16,16,128]{2,1,0:T(8,128)} %labels_in.1, f32[16]{0:T(128)} %class_perm.1, s32[16,16,128]{2,1,0:T(8,128)} %support_in.1, f32[4,2,64,32]{3,2,1,0:T(8,128)} %constant.2.clone.placing), custom_call_target="tpu_custom_call" | custom-call | tf_op jit(solution)/shard_map/pallas_call | solution.py:488
  37.8 0.0 copy-start
  37.9 2.3 %copy.9 = f32[8,16,16,128]{3,2,1,0:T(8,128)} copy(f32[8,16,16,128]{3,2,1,0:T(8,128)} %get-tuple-element.8) | data formatting | bytes 2097152
  40.1 0.0 copy-done
  40.1 0.6 %copy.10 = f32[27,1,1,8]{0,3,2,1:T(8,128)} copy(f32[27,1,1,8]{0,3,2,1:T(8,128)S(1)} %bitcast.3) | data formatting | bytes 1728
Async XLA Ops:
  37.8 2.3 %copy-start = (f32[8,27]{1,0:T(8,128)S(1)}, f32[8,27]{1,0:T(8,128)}, u32[]{:S(2)}) copy-start(f32[8,27]{1,0:T(8,128)} %get-tuple-element.5) | copy-start | bytes 2596

commit v6 on v5

--- a/solution.py
+++ b/solution.py
@@ -136,6 +136,12 @@
     def has_device(x, y):
         return (x >= 0) & (x < nx) & (y >= 0) & (y < ny)
 
+    barrier = pltpu.get_barrier_semaphore()
+    for dx, dy in directions:
+        @pl.when(has_device(gi + dx, gj + dy))
+        def _():
+            pl.semaphore_signal(barrier, 1, device_id=(gi + dx, gj + dy), device_id_type=mesh_id)
+
     def pieces(dx, dy):
         return [(0, run) for run in slot_runs(shared_slots(dx, dy))] + [(1, None), (2, None)]
 
@@ -184,12 +190,6 @@
         def _():
             received[k] = jnp.zeros(received.shape[1:], received.dtype)
 
-    barrier = pltpu.get_barrier_semaphore()
-    for dx, dy in directions:
-        @pl.when(has_device(gi + dx, gj + dy))
-        def _():
-            pl.semaphore_signal(barrier, 1, device_id=(gi + dx, gj + dy), device_id_type=mesh_id)
-
     pl.semaphore_wait(barrier, peers)
 
     def remote_copy(k, p, dx, dy, target_x, target_y):
@@ -211,18 +211,20 @@
             for p in range(len(pieces(dx, dy))):
                 remote_copy(k, p, dx, dy, gi + dx, gj + dy).start()
 
-    for local_copy in local_copies:
-        local_copy.wait()
-    for k, (dx, dy) in enumerate(directions):
-        @pl.when(has_device(gi + dx, gj + dy))
-        def _():
-            for p in range(len(pieces(dx, dy))):
-                remote_copy(k, p, dx, dy, gi + dx, gj + dy).wait_send()
-
-        @pl.when(has_device(gi - dx, gj - dy))
-        def _():
-            for p in range(len(pieces(dx, dy))):
-                remote_copy(k, p, dx, dy, gi - dx, gj - dy).wait_recv()
+    def wait_halo(chosen):
+        for k, (dx, dy) in enumerate(directions):
+            if not chosen(dx, dy):
+                continue
+
+            @pl.when(has_device(gi + dx, gj + dy))
+            def _():
+                for p in range(len(pieces(dx, dy))):
+                    remote_copy(k, p, dx, dy, gi + dx, gj + dy).wait_send()
+
+            @pl.when(has_device(gi - dx, gj - dy))
+            def _():
+                for p in range(len(pieces(dx, dy))):
+                    remote_copy(k, p, dx, dy, gi - dx, gj - dy).wait_recv()
 
     row = lax.broadcasted_iota(jnp.int32, (YE, L), 0)
     lane = lax.broadcasted_iota(jnp.int32, (YE, L), 1)
@@ -248,7 +250,10 @@
         pm[x] = jnp.where(inside, perm, 0.0)
         return carry
 
-    lax.fori_loop(0, XE, lookup, 0)
+    for local_copy in local_copies:
+        local_copy.wait()
+    wait_halo(lambda dx, dy: dx == 0)
+    lax.fori_loop(HX, HX + NXL, lookup, 0)
 
     def xplace(x):
         return (x + (CB - HX)) & (CB - 1)
@@ -300,7 +305,12 @@
             wa[s, x] = eb[s, x] * v
         return carry
 
-    lax.fori_loop(0, XE, pre, 0)
+    lax.fori_loop(HX + 1, HX + NXL - 1, pre, 0)
+    wait_halo(lambda dx, dy: dx != 0)
+    lax.fori_loop(0, HX, lookup, 0)
+    lax.fori_loop(HX + NXL, XE, lookup, 0)
+    lax.fori_loop(0, HX + 1, pre, 0)
+    lax.fori_loop(HX + NXL - 1, XE, pre, 0)
 
     def inflow_of(src, x, s, c):
         bx, by, bz = corner_of(s)

time: 41.1 us -> 39.3 us (0.956)
  Pallas kernels: 37.2 us -> 35.3 us
    pallas_call x1, Pallas kernels: 37.2 us -> 35.3 us  [shards(): pl.pallas_call(functools.partial(smooth_kernel, nx, ny), out_shape=(jax.S...]
where the time goes in v6:
time: 39.3 us; the launch traced here: 38.8 us
  Pallas kernels  35.3 us (90%)
  local copies, waits for them, and re-layouts  2.87 us (7%)
  between operations  0.65 us (2%)
    pallas_call x1, Pallas kernels, shards(): pl.pallas_call(functools.partial(smooth_kernel, nx, ny), out_shape=(jax.S...  35.3 us
    unnamed x4, local copies, waits for them, and re-layouts  2.87 us

profile of v6, /device:TPU:70, one launch (start us, length us, event | category | flops | bytes accessed | tf_op | source)
XLA Modules:
  0.0 38.8 jit_solution(7485838089581094957)
XLA Ops:
  0.6 35.3 %shard_map.68 = (f32[8,16,16,128]{3,2,1,0:T(8,128)}, f32[8,27]{1,0:T(8,128)}) custom-call(f32[8,16,16,128]{3,2,1,0:T(8,128)} %basis_in.1, s32[16,16,128]{2,1,0:T(8,128)} %labels_in.1, f32[16]{0:T(128)} %class_perm.1, s32[16,16,128]{2,1,0:T(8,128)} %support_in.1, f32[4,2,64,32]{3,2,1,0:T(8,128)} %constant.2.clone.placing), custom_call_target="tpu_custom_call" | custom-call | tf_op jit(solution)/shard_map/pallas_call | solution.py:498
  36.0 0.0 copy-start
  36.0 2.3 %copy.9 = f32[8,16,16,128]{3,2,1,0:T(8,128)} copy(f32[8,16,16,128]{3,2,1,0:T(8,128)} %get-tuple-element.8) | data formatting | bytes 2097152
  38.3 0.0 copy-done
  38.3 0.6 %copy.10 = f32[27,1,1,8]{0,3,2,1:T(8,128)} copy(f32[27,1,1,8]{0,3,2,1:T(8,128)S(1)} %bitcast.3) | data formatting | bytes 1728
Async XLA Ops:
  36.0 2.3 %copy-start = (f32[8,27]{1,0:T(8,128)S(1)}, f32[8,27]{1,0:T(8,128)}, u32[]{:S(2)}) copy-start(f32[8,27]{1,0:T(8,128)} %get-tuple-element.5) | copy-start | bytes 2596

commit v7 on v6

--- a/solution.py
+++ b/solution.py
@@ -289,6 +289,9 @@
         tt[9, x] = jnp.where(m_zhi, 0.0, t_zp)
         tt[10, x] = t_zm
         tt[11, x] = jnp.where(m_zlo, 0.0, t_zm)
+        return carry
+
+    def pre_w(x, carry):
         sup = es[x]
         node_x = gi + ((x + (CB - HX)) >> 4) < nx
         for s in range(8):
@@ -305,12 +308,8 @@
             wa[s, x] = eb[s, x] * v
         return carry
 
+    lax.fori_loop(HX, HX + NXL, pre_w, 0)
     lax.fori_loop(HX + 1, HX + NXL - 1, pre, 0)
-    wait_halo(lambda dx, dy: dx != 0)
-    lax.fori_loop(0, HX, lookup, 0)
-    lax.fori_loop(HX + NXL, XE, lookup, 0)
-    lax.fori_loop(0, HX + 1, pre, 0)
-    lax.fori_loop(HX + NXL - 1, XE, pre, 0)
 
     def inflow_of(src, x, s, c):
         bx, by, bz = corner_of(s)
@@ -362,7 +361,17 @@
 
     bufs = (wa, wb)
     for step in range(ITERS):
-        sweep(bufs[step % 2], bufs[(step + 1) % 2], step + 1, XE - step - 1)
+        sweep(bufs[step % 2], bufs[(step + 1) % 2], HX + step + 1, HX + NXL - step - 1)
+    wait_halo(lambda dx, dy: dx != 0)
+    lax.fori_loop(0, HX, lookup, 0)
+    lax.fori_loop(HX + NXL, XE, lookup, 0)
+    lax.fori_loop(0, HX, pre_w, 0)
+    lax.fori_loop(HX + NXL, XE, pre_w, 0)
+    lax.fori_loop(0, HX + 1, pre, 0)
+    lax.fori_loop(HX + NXL - 1, XE, pre, 0)
+    for step in range(ITERS):
+        sweep(bufs[step % 2], bufs[(step + 1) % 2], step + 1, HX + step + 1)
+        sweep(bufs[step % 2], bufs[(step + 1) % 2], HX + NXL - step - 1, XE - step - 1)
     last = bufs[ITERS % 2]
     basis_buf = wc
 

time: 39.3 us -> 38.1 us (0.969)
  Pallas kernels: 35.3 us -> 34.5 us
    pallas_call x1, Pallas kernels: 35.3 us -> 34.5 us  [shards(): pl.pallas_call(functools.partial(smooth_kernel, nx, ny), out_shape=(jax.S...]
where the time goes in v7:
time: 38.1 us; the launch traced here: 38 us
  Pallas kernels  34.5 us (91%)
  local copies, waits for them, and re-layouts  2.87 us (8%)
  between operations  0.65 us (2%)
    pallas_call x1, Pallas kernels, shards(): pl.pallas_call(functools.partial(smooth_kernel, nx, ny), out_shape=(jax.S...  34.5 us
    unnamed x4, local copies, waits for them, and re-layouts  2.87 us

profile of v7, /device:TPU:70, one launch (start us, length us, event | category | flops | bytes accessed | tf_op | source)
XLA Modules:
  0.0 38.0 jit_solution(18032452101211838994)
XLA Ops:
  0.6 34.5 %shard_map.68 = (f32[8,16,16,128]{3,2,1,0:T(8,128)}, f32[8,27]{1,0:T(8,128)}) custom-call(f32[8,16,16,128]{3,2,1,0:T(8,128)} %basis_in.1, s32[16,16,128]{2,1,0:T(8,128)} %labels_in.1, f32[16]{0:T(128)} %class_perm.1, s32[16,16,128]{2,1,0:T(8,128)} %support_in.1, f32[4,2,64,32]{3,2,1,0:T(8,128)} %constant.2.clone.placing), custom_call_target="tpu_custom_call" | custom-call | tf_op jit(solution)/shard_map/pallas_call | solution.py:507
  35.1 0.0 copy-start
  35.1 2.3 %copy.9 = f32[8,16,16,128]{3,2,1,0:T(8,128)} copy(f32[8,16,16,128]{3,2,1,0:T(8,128)} %get-tuple-element.8) | data formatting | bytes 2097152
  37.4 0.0 copy-done
  37.4 0.6 %copy.10 = f32[27,1,1,8]{0,3,2,1:T(8,128)} copy(f32[27,1,1,8]{0,3,2,1:T(8,128)S(1)} %bitcast.3) | data formatting | bytes 1728
Async XLA Ops:
  35.1 2.3 %copy-start = (f32[8,27]{1,0:T(8,128)S(1)}, f32[8,27]{1,0:T(8,128)}, u32[]{:S(2)}) copy-start(f32[8,27]{1,0:T(8,128)} %get-tuple-element.5) | copy-start | bytes 2596

commit v8 on v7

--- a/solution.py
+++ b/solution.py
@@ -426,7 +426,7 @@
 
     lax.fori_loop(HX, HX + NXL, image, 0)
 
-    for s1 in range(8):
+    def pair_rows(s1):
         def pair_sums(x, acc):
             b = basis_buf[s1, x + HX]
             return tuple(acc[s2] + b * img[s2, x] for s2 in range(8))
@@ -442,17 +442,19 @@
     block = lax.broadcasted_iota(jnp.int32, (nbz, L), 1) >> 4
     same_node = jnp.where(block == node, 1.0, 0.0)
     node_above = jnp.where(block + 1 == node, 1.0, 0.0)
-    pairs = prod_ref[...]
     along_lanes = (((1,), (1,)), ((), ()))
     exact = lax.Precision.HIGHEST
-    low = lax.dot_general(same_node, pairs, along_lanes, precision=exact,
-                          preferred_element_type=jnp.float32)
-    high = lax.dot_general(node_above, pairs, along_lanes, precision=exact,
-                           preferred_element_type=jnp.float32)
-    for c in range(4):
-        terms[c] = jnp.dot(low, placing[c, 0], precision=exact,
+
+    def class_terms(c):
+        rows = pl.ds(16 * c, 16)
+        pairs = prod_ref[rows, :]
+        low = lax.dot_general(same_node, pairs, along_lanes, precision=exact,
+                              preferred_element_type=jnp.float32)
+        high = lax.dot_general(node_above, pairs, along_lanes, precision=exact,
+                               preferred_element_type=jnp.float32)
+        terms[c] = jnp.dot(low, placing[c, 0, rows, :], precision=exact,
                            preferred_element_type=jnp.float32) + jnp.dot(
-            high, placing[c, 1], precision=exact, preferred_element_type=jnp.float32)
+            high, placing[c, 1, rows, :], precision=exact, preferred_element_type=jnp.float32)
 
     def coarse_copy(k, c, target_x, target_y):
         return pltpu.make_async_remote_copy(
@@ -464,10 +466,18 @@
             device_id_type=mesh_id,
         )
 
+    for s1 in range(2, 8):
+        pair_rows(s1)
+    for c in range(1, 4):
+        class_terms(c)
     for k, (c, dx, dy) in enumerate(coarse_routes):
         @pl.when(has_device(gi + dx, gj + dy))
         def _():
             coarse_copy(k, c, gi + dx, gj + dy).start()
+
+    for s1 in range(2):
+        pair_rows(s1)
+    class_terms(0)
 
     for k, (c, dx, dy) in enumerate(coarse_routes):
         @pl.when(has_device(gi + dx, gj + dy))

time: 38.1 us -> 37.8 us (level)
  no operation moved by 1% of the time
where the time goes in v8:
time: 37.8 us; the launch traced here: 37.7 us
  Pallas kernels  34.2 us (90%)
  local copies, waits for them, and re-layouts  2.87 us (8%)
  between operations  0.65 us (2%)
    pallas_call x1, Pallas kernels, shards(): pl.pallas_call(functools.partial(smooth_kernel, nx, ny), out_shape=(jax.S...  34.2 us
    unnamed x4, local copies, waits for them, and re-layouts  2.87 us

profile of v8, /device:TPU:70, one launch (start us, length us, event | category | flops | bytes accessed | tf_op | source)
XLA Modules:
  0.0 37.7 jit_solution(17197164024377633925)
XLA Ops:
  0.6 34.2 %shard_map.68 = (f32[8,16,16,128]{3,2,1,0:T(8,128)}, f32[8,27]{1,0:T(8,128)}) custom-call(f32[8,16,16,128]{3,2,1,0:T(8,128)} %basis_in.1, s32[16,16,128]{2,1,0:T(8,128)} %labels_in.1, f32[16]{0:T(128)} %class_perm.1, s32[16,16,128]{2,1,0:T(8,128)} %support_in.1, f32[4,2,64,32]{3,2,1,0:T(8,128)} %constant.2.clone.placing), custom_call_target="tpu_custom_call" | custom-call | tf_op jit(solution)/shard_map/pallas_call | solution.py:517
  34.8 0.0 copy-start
  34.8 2.3 %copy.9 = f32[8,16,16,128]{3,2,1,0:T(8,128)} copy(f32[8,16,16,128]{3,2,1,0:T(8,128)} %get-tuple-element.8) | data formatting | bytes 2097152
  37.1 0.0 copy-done
  37.1 0.6 %copy.10 = f32[27,1,1,8]{0,3,2,1:T(8,128)} copy(f32[27,1,1,8]{0,3,2,1:T(8,128)S(1)} %bitcast.3) | data formatting | bytes 1728
Async XLA Ops:
  34.8 2.3 %copy-start = (f32[8,27]{1,0:T(8,128)S(1)}, f32[8,27]{1,0:T(8,128)}, u32[]{:S(2)}) copy-start(f32[8,27]{1,0:T(8,128)} %get-tuple-element.5) | copy-start | bytes 2596

commit v9 on v8

--- a/solution.py
+++ b/solution.py
@@ -112,7 +112,7 @@
 def smooth_kernel(
     nx, ny,
     basis_in, labels_in, class_perm, support_in, placing, basis_ref, coarse_ref,
-    eb, el, es, pm, tt, aux, valid, wa, wb, wc, img, prod_ref, terms, received,
+    eb, el, es, pm, tt, ts, aux, valid, wa, wb, wc, img, prod_ref, terms, received,
     send_sem, recv_sem, local_sem, coarse_send, coarse_recv, edge_send, edge_recv,
 ):
     gi = lax.axis_index("gx")
@@ -273,22 +273,20 @@
         t_zp = jnp.where(lane == L - 1, 0.0, conductance(pc, pzp))
         t_zm = jnp.where(lane == 0, 0.0, conductance(pc, pzm))
         diag = t_xp + t_xm + t_yp + t_ym + t_zp + t_zm
+        inv = 1.0 / jnp.where(diag > 0.0, diag, 1.0)
         aux[0, x] = diag
-        aux[1, x] = 1.0 / jnp.where(diag > 0.0, diag, 1.0)
+        aux[1, x] = 1.0 - omega_jacobi * diag * inv
+        scale = omega_jacobi * inv
         cx_hi = xplace(x) == CB - 1
         cx_lo = xplace(x) == 0
-        tt[0, x] = t_xp
-        tt[1, x] = jnp.where(cx_hi, 0.0, t_xp)
-        tt[2, x] = t_xm
-        tt[3, x] = jnp.where(cx_lo, 0.0, t_xm)
-        tt[4, x] = t_yp
-        tt[5, x] = jnp.where(m_yhi, 0.0, t_yp)
-        tt[6, x] = t_ym
-        tt[7, x] = jnp.where(m_ylo, 0.0, t_ym)
-        tt[8, x] = t_zp
-        tt[9, x] = jnp.where(m_zhi, 0.0, t_zp)
-        tt[10, x] = t_zm
-        tt[11, x] = jnp.where(m_zlo, 0.0, t_zm)
+        faces_t = (
+            t_xp, jnp.where(cx_hi, 0.0, t_xp), t_xm, jnp.where(cx_lo, 0.0, t_xm),
+            t_yp, jnp.where(m_yhi, 0.0, t_yp), t_ym, jnp.where(m_ylo, 0.0, t_ym),
+            t_zp, jnp.where(m_zhi, 0.0, t_zp), t_zm, jnp.where(m_zlo, 0.0, t_zm),
+        )
+        for f, t in enumerate(faces_t):
+            tt[f, x] = t
+            ts[f, x] = t * scale
         return carry
 
     def pre_w(x, carry):
@@ -311,7 +309,7 @@
     lax.fori_loop(HX, HX + NXL, pre_w, 0)
     lax.fori_loop(HX + 1, HX + NXL - 1, pre, 0)
 
-    def inflow_of(src, x, s, c):
+    def inflow_of(src, x, s, c, tt=tt):
         bx, by, bz = corner_of(s)
         cx_hi = xplace(x) == CB - 1
         cx_lo = xplace(x) == 0
@@ -349,12 +347,11 @@
 
     def sweep(src, dst, lo, hi):
         def body(x, carry):
-            diag = aux[0, x]
-            inv = aux[1, x]
+            keep = aux[1, x]
             for s in range(8):
                 c = src[s, x]
-                inflow = inflow_of(src, x, s, c)
-                dst[s, x] = (c - omega_jacobi * (diag * c - inflow) * inv) * valid[s, x]
+                inflow = inflow_of(src, x, s, c, ts)
+                dst[s, x] = (c * keep + inflow) * valid[s, x]
             return carry
 
         lax.fori_loop(lo, hi, body, 0)
@@ -528,6 +525,7 @@
             pltpu.VMEM((XE, YE, size_z), jnp.int32),
             pltpu.VMEM((XE, YE, size_z), f32),
             pltpu.VMEM((12, XE, YE, size_z), f32),
+            pltpu.VMEM((12, XE, YE, size_z), f32),
             pltpu.VMEM((2, XE, YE, size_z), f32),
             pltpu.VMEM((8, XE, YE, size_z), f32),
             pltpu.VMEM((8, XE, YE, size_z), f32),

time: 37.8 us -> 37.9 us (level)
  no operation moved by 1% of the time
where the time goes in v9:
time: 37.9 us; the launch traced here: 37.7 us
  Pallas kernels  34.2 us (90%)
  local copies, waits for them, and re-layouts  2.87 us (8%)
  between operations  0.65 us (2%)
    pallas_call x1, Pallas kernels, shards(): pl.pallas_call(functools.partial(smooth_kernel, nx, ny), out_shape=(jax.S...  34.2 us
    unnamed x4, local copies, waits for them, and re-layouts  2.87 us

profile of v9, /device:TPU:70, one launch (start us, length us, event | category | flops | bytes accessed | tf_op | source)
XLA Modules:
  0.0 37.7 jit_solution(15192822609730510537)
XLA Ops:
  0.6 34.2 %shard_map.68 = (f32[8,16,16,128]{3,2,1,0:T(8,128)}, f32[8,27]{1,0:T(8,128)}) custom-call(f32[8,16,16,128]{3,2,1,0:T(8,128)} %basis_in.1, s32[16,16,128]{2,1,0:T(8,128)} %labels_in.1, f32[16]{0:T(128)} %class_perm.1, s32[16,16,128]{2,1,0:T(8,128)} %support_in.1, f32[4,2,64,32]{3,2,1,0:T(8,128)} %constant.2.clone.placing), custom_call_target="tpu_custom_call" | custom-call | tf_op jit(solution)/shard_map/pallas_call | solution.py:514
  34.9 0.0 copy-start
  34.9 2.3 %copy.9 = f32[8,16,16,128]{3,2,1,0:T(8,128)} copy(f32[8,16,16,128]{3,2,1,0:T(8,128)} %get-tuple-element.8) | data formatting | bytes 2097152
  37.1 0.0 copy-done
  37.1 0.6 %copy.10 = f32[27,1,1,8]{0,3,2,1:T(8,128)} copy(f32[27,1,1,8]{0,3,2,1:T(8,128)S(1)} %bitcast.3) | data formatting | bytes 1728
Async XLA Ops:
  34.9 2.3 %copy-start = (f32[8,27]{1,0:T(8,128)S(1)}, f32[8,27]{1,0:T(8,128)}, u32[]{:S(2)}) copy-start(f32[8,27]{1,0:T(8,128)} %get-tuple-element.5) | copy-start | bytes 2596

commit v10 on v9

--- a/solution.py
+++ b/solution.py
@@ -383,6 +383,10 @@
         return carry
 
     lax.fori_loop(HX, HX + NXL, normalize, 0)
+    out_copy = pltpu.make_async_copy(
+        wc.at[:, pl.ds(HX, NXL), pl.ds(0, NYL), :], basis_ref, local_sem.at[3]
+    )
+    out_copy.start()
 
     def edge_copy(k, p, dx, dy, target_x, target_y):
         run, from_x, to_x, from_y, to_y = edge_pieces(dx, dy)[p]
@@ -418,7 +422,6 @@
             c = basis_buf[s, x]
             inflow = inflow_of(basis_buf, x, s, c)
             img[s, x - HX] = jnp.where(m_rows, diag * c - inflow, 0.0)
-            basis_ref[s, x - HX] = c[:NYL, :]
         return carry
 
     lax.fori_loop(HX, HX + NXL, image, 0)
@@ -485,6 +488,7 @@
         def _():
             coarse_copy(k, c, gi - dx, gj - dy).wait_recv()
 
+    out_copy.wait()
     total = terms[0] + received[0] + received[1] + received[2]
     coarse_ref[...] = total[:, : coarse_ref.shape[1]]
 
@@ -518,7 +522,7 @@
             jax.ShapeDtypeStruct((blocks_z, 27), f32),
         ),
         in_specs=[vmem, vmem, pl.BlockSpec(memory_space=pltpu.SMEM), vmem, vmem],
-        out_specs=(vmem, vmem),
+        out_specs=(pl.BlockSpec(memory_space=pl.ANY), vmem),
         scratch_shapes=[
             pltpu.VMEM((8, XE, YE, size_z), f32),
             pltpu.VMEM((XE, YE, size_z), jnp.int32),
@@ -537,7 +541,7 @@
             pltpu.VMEM((3, blocks_z, 32), f32),
             pltpu.SemaphoreType.DMA((32,)),
             pltpu.SemaphoreType.DMA((32,)),
-            pltpu.SemaphoreType.DMA((3,)),
+            pltpu.SemaphoreType.DMA((4,)),
             pltpu.SemaphoreType.DMA((3,)),
             pltpu.SemaphoreType.DMA((3,)),
             pltpu.SemaphoreType.DMA((8,)),

time: 37.9 us -> 37.4 us (0.987)
  Pallas kernels: 34.2 us -> 33.8 us
    pallas_call x1, Pallas kernels: 34.2 us -> 33.8 us  [shards(): pl.pallas_call(functools.partial(smooth_kernel, nx, ny), out_shape=(jax.S...]
where the time goes in v10:
time: 37.4 us; the launch traced here: 37.3 us
  Pallas kernels  33.8 us (90%)
  local copies, waits for them, and re-layouts  2.87 us (8%)
  between operations  0.65 us (2%)
    pallas_call x1, Pallas kernels, shards(): pl.pallas_call(functools.partial(smooth_kernel, nx, ny), out_shape=(jax.S...  33.8 us
    unnamed x4, local copies, waits for them, and re-layouts  2.87 us

profile of v10, /device:TPU:70, one launch (start us, length us, event | category | flops | bytes accessed | tf_op | source)
XLA Modules:
  0.0 37.3 jit_solution(1985681730156931803)
XLA Ops:
  0.6 33.8 %shard_map.68 = (f32[8,16,16,128]{3,2,1,0:T(8,128)}, f32[8,27]{1,0:T(8,128)}) custom-call(f32[8,16,16,128]{3,2,1,0:T(8,128)} %basis_in.1, s32[16,16,128]{2,1,0:T(8,128)} %labels_in.1, f32[16]{0:T(128)} %class_perm.1, s32[16,16,128]{2,1,0:T(8,128)} %support_in.1, f32[4,2,64,32]{3,2,1,0:T(8,128)} %constant.2.clone.placing), custom_call_target="tpu_custom_call" | custom-call | tf_op jit(solution)/shard_map/pallas_call | solution.py:518
  34.4 0.0 copy-start
  34.5 2.3 %copy.9 = f32[8,16,16,128]{3,2,1,0:T(8,128)} copy(f32[8,16,16,128]{3,2,1,0:T(8,128)} %get-tuple-element.8) | data formatting | bytes 2097152
  36.7 0.0 copy-done
  36.7 0.6 %copy.10 = f32[27,1,1,8]{0,3,2,1:T(8,128)} copy(f32[27,1,1,8]{0,3,2,1:T(8,128)S(1)} %bitcast.3) | data formatting | bytes 1728
Async XLA Ops:
  34.4 2.3 %copy-start = (f32[8,27]{1,0:T(8,128)S(1)}, f32[8,27]{1,0:T(8,128)}, u32[]{:S(2)}) copy-start(f32[8,27]{1,0:T(8,128)} %get-tuple-element.5) | copy-start | bytes 2596

commit v11 on v10

--- a/solution.py
+++ b/solution.py
@@ -514,6 +514,7 @@
     YE = -(-(size_y + 2 * HY) // 8) * 8
     f32 = jnp.float32
     vmem = pl.BlockSpec(memory_space=pltpu.VMEM)
+    hbm = pl.BlockSpec(memory_space=pl.ANY)
     blocks_z = size_z // CB
     basis, coarse = pl.pallas_call(
         functools.partial(smooth_kernel, nx, ny),
@@ -521,7 +522,7 @@
             jax.ShapeDtypeStruct((8, size_x, size_y, size_z), f32),
             jax.ShapeDtypeStruct((blocks_z, 27), f32),
         ),
-        in_specs=[vmem, vmem, pl.BlockSpec(memory_space=pltpu.SMEM), vmem, vmem],
+        in_specs=[hbm, hbm, pl.BlockSpec(memory_space=pltpu.SMEM), hbm, vmem],
         out_specs=(pl.BlockSpec(memory_space=pl.ANY), vmem),
         scratch_shapes=[
             pltpu.VMEM((8, XE, YE, size_z), f32),

time: 37.4 us -> 37.2 us (level)
  no operation moved by 1% of the time
where the time goes in v11:
time: 37.2 us; the launch traced here: 37.1 us
  Pallas kernels  33.6 us (90%)
  local copies, waits for them, and re-layouts  2.87 us (8%)
  between operations  0.65 us (2%)
    pallas_call x1, Pallas kernels, shards(): pl.pallas_call(functools.partial(smooth_kernel, nx, ny), out_shape=(jax.S...  33.6 us
    unnamed x4, local copies, waits for them, and re-layouts  2.87 us

profile of v11, /device:TPU:70, one launch (start us, length us, event | category | flops | bytes accessed | tf_op | source)
XLA Modules:
  0.0 37.1 jit_solution(7604677791679475881)
XLA Ops:
  0.6 33.6 %shard_map.68 = (f32[8,16,16,128]{3,2,1,0:T(8,128)}, f32[8,27]{1,0:T(8,128)}) custom-call(f32[8,16,16,128]{3,2,1,0:T(8,128)} %basis_in.1, s32[16,16,128]{2,1,0:T(8,128)} %labels_in.1, f32[16]{0:T(128)} %class_perm.1, s32[16,16,128]{2,1,0:T(8,128)} %support_in.1, f32[4,2,64,32]{3,2,1,0:T(8,128)} %constant.2.clone.placing), custom_call_target="tpu_custom_call" | custom-call | tf_op jit(solution)/shard_map/pallas_call | solution.py:519
  34.2 0.0 copy-start
  34.2 2.3 %copy.9 = f32[8,16,16,128]{3,2,1,0:T(8,128)} copy(f32[8,16,16,128]{3,2,1,0:T(8,128)} %get-tuple-element.8) | data formatting | bytes 2097152
  36.5 0.0 copy-done
  36.5 0.6 %copy.10 = f32[27,1,1,8]{0,3,2,1:T(8,128)} copy(f32[27,1,1,8]{0,3,2,1:T(8,128)S(1)} %bitcast.3) | data formatting | bytes 1728
Async XLA Ops:
  34.2 2.3 %copy-start = (f32[8,27]{1,0:T(8,128)S(1)}, f32[8,27]{1,0:T(8,128)}, u32[]{:S(2)}) copy-start(f32[8,27]{1,0:T(8,128)} %get-tuple-element.5) | copy-start | bytes 2596

commit v12 on v11

--- a/solution.py
+++ b/solution.py
@@ -382,11 +382,8 @@
             basis_buf[s, x, pl.ds(0, NYL), :] = (vals[s] / scale)[:NYL, :]
         return carry
 
-    lax.fori_loop(HX, HX + NXL, normalize, 0)
-    out_copy = pltpu.make_async_copy(
-        wc.at[:, pl.ds(HX, NXL), pl.ds(0, NYL), :], basis_ref, local_sem.at[3]
-    )
-    out_copy.start()
+    lax.fori_loop(HX, HX + 1, normalize, 0)
+    lax.fori_loop(HX + NXL - 1, HX + NXL, normalize, 0)
 
     def edge_copy(k, p, dx, dy, target_x, target_y):
         run, from_x, to_x, from_y, to_y = edge_pieces(dx, dy)[p]
@@ -400,6 +397,22 @@
         )
 
     for k, (dx, dy) in enumerate(faces):
+        if dy != 0:
+            continue
+
+        @pl.when(has_device(gi + dx, gj + dy))
+        def _():
+            for p in range(len(edge_pieces(dx, dy))):
+                edge_copy(k, p, dx, dy, gi + dx, gj + dy).start()
+    lax.fori_loop(HX + 1, HX + NXL - 1, normalize, 0)
+    out_copy = pltpu.make_async_copy(
+        wc.at[:, pl.ds(HX, NXL), pl.ds(0, NYL), :], basis_ref, local_sem.at[3]
+    )
+    out_copy.start()
+    for k, (dx, dy) in enumerate(faces):
+        if dx != 0:
+            continue
+
         @pl.when(has_device(gi + dx, gj + dy))
         def _():
             for p in range(len(edge_pieces(dx, dy))):

time: 37.2 us -> 36.9 us (level)
  no operation moved by 1% of the time
where the time goes in v12:
time: 36.9 us; the launch traced here: 36.8 us
  Pallas kernels  33.3 us (90%)
  local copies, waits for them, and re-layouts  2.87 us (8%)
  between operations  0.65 us (2%)
    pallas_call x1, Pallas kernels, shards(): pl.pallas_call(functools.partial(smooth_kernel, nx, ny), out_shape=(jax.S...  33.3 us
    unnamed x4, local copies, waits for them, and re-layouts  2.87 us

profile of v12, /device:TPU:70, one launch (start us, length us, event | category | flops | bytes accessed | tf_op | source)
XLA Modules:
  0.0 36.8 jit_solution(12077746894348030971)
XLA Ops:
  0.6 33.3 %shard_map.68 = (f32[8,16,16,128]{3,2,1,0:T(8,128)}, f32[8,27]{1,0:T(8,128)}) custom-call(f32[8,16,16,128]{3,2,1,0:T(8,128)} %basis_in.1, s32[16,16,128]{2,1,0:T(8,128)} %labels_in.1, f32[16]{0:T(128)} %class_perm.1, s32[16,16,128]{2,1,0:T(8,128)} %support_in.1, f32[4,2,64,32]{3,2,1,0:T(8,128)} %constant.2.clone.placing), custom_call_target="tpu_custom_call" | custom-call | tf_op jit(solution)/shard_map/pallas_call | solution.py:532
  33.9 0.0 copy-start
  33.9 2.3 %copy.9 = f32[8,16,16,128]{3,2,1,0:T(8,128)} copy(f32[8,16,16,128]{3,2,1,0:T(8,128)} %get-tuple-element.8) | data formatting | bytes 2097152
  36.2 0.0 copy-done
  36.2 0.6 %copy.10 = f32[27,1,1,8]{0,3,2,1:T(8,128)} copy(f32[27,1,1,8]{0,3,2,1:T(8,128)S(1)} %bitcast.3) | data formatting | bytes 1728
Async XLA Ops:
  33.9 2.3 %copy-start = (f32[8,27]{1,0:T(8,128)S(1)}, f32[8,27]{1,0:T(8,128)}, u32[]{:S(2)}) copy-start(f32[8,27]{1,0:T(8,128)} %get-tuple-element.5) | copy-start | bytes 2596
